TPU v7x, 128 devices: a whole 4x4x4 slice. The times are simulated.
128 devices in a mesh: node: 32 (over z, y_lo, x), rep: 4 (over y_hi, core).
Axes of the slice: x: 4, y: 4 (y_hi: 2, y_lo: 2; y = y_hi * 2 + y_lo), z: 4, core: 2. Of those that a mesh axis runs over, the one named last changes fastest.
Arguments:
- node_feats: bfloat16 [65536, 256], P('node'), may hold values from -6 to 6
- weight: bfloat16 [256, 256], replicated, may hold values from -0.375 to 0.375
- cotangent: bfloat16 [65536, 256], P(('node', 'rep')), may hold values from -6 to 6
- tiles: bfloat16 [32, 4, 160, 256, 256], P('node', 'rep'), may hold values from -0.049804688 to 0.049804688
- tile_rows: int32 [32, 4, 160], P('node', 'rep'), may hold values from 0 to 7
- tile_cols: int32 [32, 4, 160], P('node', 'rep'), may hold values from 0 to 63
- tile_count: int32 [32, 4], P('node', 'rep'), may hold values from 80 to 160, as said below
Outputs:
- activated: bfloat16 [65536, 256], P(('node', 'rep'))
- feature_grad: bfloat16 [65536, 256], P(('node', 'rep'))
- weight_grad: float32 [256, 256], replicated
Inputs may be any that keep to these rules, and one draw needn't show every extreme that they name: `tile_count`: slots at and beyond a device's count are ignored; some device has all 160 slots live in every draw.
All inputs are finite; a program needn't handle non-finite values.
Results may differ from a plain program's by a relative error of at most 0.007.
Values may be sent and summed in bfloat16 or wider, within the bound.
No kernel may reach another device: no remote copies, remote signals or barrier semaphores. Data moves between devices by JAX's collectives and lax.ppermute only.
A program may use at most 256 MiB of HBM per device.

v0:
```python
import functools

import jax
import jax.numpy as jnp
from jax import lax
from jax.experimental import pallas as pl
from jax.experimental.pallas import tpu as pltpu
from jax.sharding import PartitionSpec as P

AXES = ("node", "rep")
NZ, NYL, NX, NYH, NC = 4, 2, 4, 2, 2
B = 256
F32, BF16, I32 = jnp.float32, jnp.bfloat16, jnp.int32
NBUF = 32
UNROLL = 4
MIB = 1 << 20


def _flat(z, yl, x, yh, c):
    return ((((z % NZ) * NYL + yl) * NX + x % NX) * NYH + yh) * NC + c


def _perm(move):
    pairs = []
    for z in range(NZ):
        for yl in range(NYL):
            for x in range(NX):
                for yh in range(NYH):
                    for c in range(NC):
                        pairs.append((_flat(z, yl, x, yh, c), _flat(*move(z, yl, x, yh, c))))
    return pairs


def _along(first, step):
    def move(z, yl, x, yh, c):
        if (c == 0) == first:
            return z, yl, step(x), yh, c
        return step(z), yl, x, yh, c

    return _perm(move)


UP, UM, U2 = (_along(True, lambda k, d=d: k + d) for d in (1, -1, 2))
VP, VM, V2 = (_along(False, lambda k, d=d: k + d) for d in (1, -1, 2))
YN = _perm(lambda z, yl, x, yh, c: (z, 1 - yl, x, yh, c))
YH = _perm(lambda z, yl, x, yh, c: (z, yl, x, 1 - yh, c))
CC = _perm(lambda z, yl, x, yh, c: (z, yl, x, yh, 1 - c))


def send(value, pairs):
    return lax.ppermute(value, AXES, pairs)


def tie(value, *deps):
    return lax.optimization_barrier((value, *deps))[0]


def _sorted(v):
    n = v.shape[0]
    rank = jnp.sum((v[None, :] < v[:, None]).astype(I32), axis=1)
    hit = rank[:, None] == jnp.arange(n, dtype=I32)[None, :]
    return jnp.sum(jnp.where(hit, v[:, None], 0), axis=0)


def tables(rows, cols, count, z, yl, x, yh, c):
    slots = jnp.arange(rows.shape[0], dtype=I32)
    live = slots < count
    j = cols % 2
    xr = (cols // 2 % NX - x) % NX
    yr = (cols // (2 * NX) % NYL) ^ yl
    zr = (cols // (2 * NX * NYL) - z) % NZ
    ur = jnp.where(c == 0, xr, zr)
    vr = jnp.where(c == 0, zr, xr)
    at = jnp.where(ur == 0, 0, jnp.where(ur == 3, 1, jnp.where(ur == 1, 2, 3)))
    block = at * 2 + j
    h = yr
    far = jnp.where(vr == 2, 6 + h, jnp.where(vr == 3, 2 + 2 * h, h))
    seg = jnp.where(vr == 1, 3 + 2 * h, far)
    bseg = jnp.where(vr == 1, 5 - 2 * h, far)
    q = rows // 2
    rpos = ((q % 2) ^ c) * 4 + ((q // 2) ^ yh) * 2 + rows % 2
    ends = jnp.arange(9, dtype=I32)[:, None]

    def offsets(key):
        return jnp.sum((key[None, :] < ends).astype(I32), axis=1)

    fkey = jnp.where(live, seg, 8)
    bkey = jnp.where(live, (bseg // 2) * 2 + rpos // 4, 8)
    col = (bseg % 2) * 8 + block
    fwd = _sorted((fkey << 24) | (rpos << 18) | (block << 8) | slots)
    bwd = _sorted((bkey << 24) | (col << 18) | ((rpos % 4) << 8) | slots)
    return fwd, bwd, offsets(fkey), offsets(bkey)


def _run_tiles(tab, bounds, tiles, tbuf, tsem, steps, prepare):
    first, end = bounds[0], bounds[-1]

    def fetch(i):
        at = lax.rem(i, NBUF)
        return pltpu.make_async_copy(tiles.at[tab[i] & 255], tbuf.at[at], tsem.at[at])

    def start(i, carry):
        fetch(i).start()
        return carry

    def run(base, width, step):
        for u in range(width):
            fetch(base + u).wait()
        for u in range(width):
            step(tab[base + u], tbuf.at[lax.rem(base + u, NBUF)])
        for u in range(width):

            @pl.when(base + u + NBUF < end)
            def _():
                fetch(base + u + NBUF).start()

    lax.fori_loop(first, jnp.minimum(first + NBUF, end), start, 0)
    prepare()
    for lo, hi, step in zip(bounds[:-1], bounds[1:], steps):
        whole = (hi - lo) // UNROLL

        def many(g, carry, lo=lo, step=step):
            run(lo + g * UNROLL, UNROLL, step)
            return carry

        lax.fori_loop(0, whole, many, 0)
        at = lo + whole * UNROLL
        width = UNROLL // 2
        while width:
            take = ((hi - at) & width) != 0

            @pl.when(take)
            def _(at=at, width=width, step=step):
                run(at, width, step)

            at = at + jnp.where(take, width, 0)
            width //= 2


def _forward_kernel(chunk, tab, offs, tiles, fa, fb, *refs):
    if chunk:
        refs = refs[1:]
    acc, tbuf, tsem = refs

    def step(feats):
        def go(word, tile):
            r = (word >> 18) & 7
            acc[r] += jnp.dot(tile[...], feats[(word >> 8) & 7], preferred_element_type=F32)

        return go

    def prepare():
        if not chunk:
            acc[...] = jnp.zeros_like(acc)

    bounds = [offs[2 * chunk + k] for k in range(3)]
    _run_tiles(tab, bounds, tiles, tbuf, tsem, [step(fa), step(fb)], prepare)


ANY = pl.BlockSpec(memory_space=pl.ANY)
HBM = pl.BlockSpec(memory_space=pltpu.HBM)
SMEM = pl.BlockSpec(memory_space=pltpu.SMEM)
VMEM = pl.BlockSpec(memory_space=pltpu.VMEM)


def _cost(extra):
    return pl.CostEstimate(
        flops=B**3, bytes_accessed=B * B, transcendentals=0
    )


def forward(chunk, tab, offs, tiles, fa, fb, acc):
    args = [tab, offs, tiles, fa, fb] + ([acc] if chunk else [])
    return pl.pallas_call(
        functools.partial(_forward_kernel, chunk),
        name=f"tiles_forward_{chunk}",
        in_specs=[SMEM, SMEM, HBM] + [VMEM] * (len(args) - 3),
        out_specs=VMEM,
        out_shape=jax.ShapeDtypeStruct((8, B, B), F32),
        input_output_aliases={5: 0} if chunk else {},
        scratch_shapes=[
            pltpu.VMEM((NBUF, B, B), BF16),
            pltpu.SemaphoreType.DMA((NBUF,)),
        ],
        compiler_params=pltpu.CompilerParams(vmem_limit_bytes=16 * MIB),
        cost_estimate=_cost(6 * MIB),
    )(*args)


def _backward_kernel(chunk, nadd, tab, offs, tiles, d0, d1, *refs):
    adds, refs = refs[:nadd], refs[nadd:]
    oa, ob, acc, tbuf, tsem = refs

    def step(dagg):
        def go(word, tile):
            f = (word >> 18) & 15
            acc[f] += jnp.dot(dagg[(word >> 8) & 3], tile[...], preferred_element_type=F32)

        return go

    def prepare():
        if chunk == 2:
            acc[0:8] = adds[0][...].astype(F32)
            acc[8:16] = adds[1][...].astype(F32)
        else:
            acc[...] = jnp.zeros_like(acc)

    bounds = [offs[2 * chunk + k] for k in range(3)]
    _run_tiles(tab, bounds, tiles, tbuf, tsem, [step(d0), step(d1)], prepare)
    if chunk != 1:
        oa[...] = acc[0:8].astype(BF16)
        ob[...] = acc[8:16].astype(BF16)
    else:
        for k in range(8):
            oa[k * B : (k + 1) * B] = acc[k].astype(BF16)
            ob[k * B : (k + 1) * B] = acc[8 + k].astype(BF16)
        oa[8 * B :] = adds[0][...]
        ob[8 * B :] = adds[0][...]


def backward(chunk, tab, offs, tiles, d0, d1, adds=()):
    shape = (8 * B + B // 2, B) if chunk == 1 else (8, B, B)
    return pl.pallas_call(
        functools.partial(_backward_kernel, chunk, len(adds)),
        name=f"tiles_backward_{chunk}",
        in_specs=[SMEM, SMEM, HBM, VMEM, VMEM] + [VMEM] * len(adds),
        out_specs=[VMEM] * 2,
        out_shape=[jax.ShapeDtypeStruct(shape, BF16)] * 2,
        scratch_shapes=[
            pltpu.VMEM((16, B, B), F32),
            pltpu.VMEM((NBUF, B, B), BF16),
            pltpu.SemaphoreType.DMA((NBUF,)),
        ],
        compiler_params=pltpu.CompilerParams(vmem_limit_bytes=24 * MIB),
        cost_estimate=_cost(6 * MIB),
    )(tab, offs, tiles, d0, d1, *adds)


def _dense_kernel(near, far, cot0, cot1, w_ref, act, dagg, wterm):
    w = w_ref[...]
    for k in range(4):
        agg = (near[k].astype(F32) + far[(k + 2) % 4].astype(F32)).astype(BF16)
        pre = jnp.dot(agg, w, preferred_element_type=F32)
        sig = jax.nn.sigmoid(pre)
        cot = (cot0 if k < 2 else cot1)[k % 2].astype(F32)
        dpre = (cot * sig * (1.0 + pre * (1.0 - sig))).astype(BF16)
        dagg[k] = lax.dot_general(
            w, dpre, (((1,), (1,)), ((), ())), preferred_element_type=F32
        ).astype(BF16)
        term = lax.dot_general(agg, dpre, (((0,), (0,)), ((), ())), preferred_element_type=F32)
        if k < 2:
            act[k] = (pre * sig).astype(BF16)
        if k % 2 == 0:
            wterm[k // 2] = term
        else:
            wterm[k // 2] = wterm[k // 2] + term


def dense(near, far, cot0, cot1, w):
    return pl.pallas_call(
        _dense_kernel,
        name="dense",
        in_specs=[VMEM] * 5,
        out_specs=[VMEM] * 3,
        out_shape=[
            jax.ShapeDtypeStruct((2, B, B), BF16),
            jax.ShapeDtypeStruct((4, B, B), BF16),
            jax.ShapeDtypeStruct((2, B, B), F32),
        ],
        compiler_params=pltpu.CompilerParams(vmem_limit_bytes=16 * MIB),
        cost_estimate=pl.CostEstimate(
            flops=10 * 2 * B**3, bytes_accessed=5 * MIB, transcendentals=1024 * 256
        ),
    )(near, far, cot0, cot1, w)


def plus(*terms):
    total = terms[0].astype(F32)
    for t in terms[1:]:
        total = total + t.astype(F32)
    return total.astype(BF16)


def blocks(rows):
    return rows.reshape(-1, B, B)


def carry(value, w):
    return jnp.concatenate([value.reshape(-1, B), w])


def ring_sum(own, across, left, right, kind=BF16):
    own, across, left, right = (t.astype(F32) for t in (own, across, left, right))
    return ((own + across) + (left + right)).astype(kind)


def body(node_feats, weight, cotangent, tiles, tile_rows, tile_cols, tile_count):
    node, rep = lax.axis_index("node"), lax.axis_index("rep")
    x, yl, z = node % NX, node // NX % NYL, node // (NX * NYL)
    c, yh = rep % NC, rep // NC
    tiles = pltpu.with_memory_space_constraint(tiles[0, 0], pltpu.HBM)
    fwd, bwd, foffs, boffs = tables(
        tile_rows[0, 0], tile_cols[0, 0], tile_count[0, 0], z, yl, x, yh, c
    )
    own = lax.dynamic_slice_in_dim(node_feats.reshape(8, B, B), rep * 2, 2, 0)
    cot0 = cotangent.reshape(2, B, B)

    def ring(t):
        return jnp.concatenate([t, send(t, UP), send(t, UM), send(t, U2)])

    other = send(own, YN)
    lo, hi = ring(own), ring(other)
    cot1 = send(tie(cot0, other), YH)
    hi, cot1 = lax.optimization_barrier((hi, cot1))
    p1, m1 = send(lo, VP), send(lo, VM)
    p2, m2 = send(hi, VP), send(hi, VM)
    acc = forward(0, fwd, foffs, tiles, lo, hi, None)
    p1, m1, acc = lax.optimization_barrier((p1, m1, acc))
    p3 = send(p1, VP)
    acc = forward(1, fwd, foffs, tiles, p1, m1, acc)
    p2, m2, acc = lax.optimization_barrier((p2, m2, acc))
    m3 = send(m2, VM)
    acc = forward(2, fwd, foffs, tiles, p2, m2, acc)
    acc = forward(3, fwd, foffs, tiles, p3, m3, acc)

    core = send(acc[4:], CC)
    part = (acc[:4] + core).astype(BF16)
    across = send(part, YH)
    act, d0, term = dense(part, across, cot0, cot1, weight)

    half = B // 2
    whole = term[0] + term[1]
    keep = lax.dynamic_slice_in_dim(whole, c * half, half, 0)
    give = lax.dynamic_slice_in_dim(whole, (1 - c) * half, half, 0)
    d1, got = lax.optimization_barrier((send(d0, CC), send(give, CC)))
    w = keep + got

    fa, fb = backward(3, bwd, boffs, tiles, d0, d1)
    ra, rb = send(fa, VP), send(fb, VM)
    d0, d1, fa, fb, w = lax.optimization_barrier((d0, d1, fa, fb, w))
    w1 = send(w, YN)
    lo, hi = backward(0, bwd, boffs, tiles, d0, d1)
    d0, d1, lo, hi, w1 = lax.optimization_barrier((d0, d1, lo, hi, w1))
    w = (w + w1).astype(BF16)
    w2 = send(w, V2)
    m1, p1 = backward(1, bwd, boffs, tiles, d0, d1, (w,))
    s_hi, s_lo = send(p1, VP), send(m1, VM)
    d0, d1, m1, p1, ra, rb = lax.optimization_barrier((d0, d1, m1, p1, ra, rb))
    m2, p2 = backward(2, bwd, boffs, tiles, d0, d1, (rb, ra))
    t_lo, t_hi = send(p2, VP), send(m2, VM)
    s_lo, s_hi, w2 = lax.optimization_barrier((s_lo, s_hi, w2))
    w = ring_sum(w, w2, s_hi[8 * B :], s_lo[8 * B :])
    s_lo, s_hi = blocks(s_lo[: 8 * B]), blocks(s_hi[: 8 * B])
    def spread(own, s, t, extra):
        near, down, up, two = (plus(own[k : k + 2], s[k : k + 2], t[k : k + 2]) for k in (0, 2, 4, 6))
        if extra is not None:
            down, up, two = (carry(v, extra) for v in (down, up, two))
        return near, send(two, U2), send(up, UP), send(down, UM)

    far, *rest = spread(hi, s_hi, t_hi, w)
    near, *parts = spread(lo, s_lo, t_lo, None)
    far = plus(far, *(blocks(r[: 2 * B]) for r in rest))
    w = ring_sum(w, *(r[2 * B :] for r in rest), F32)
    other = send(far, YN)
    got = send(w, CC)
    total = sum((t.astype(F32) for t in (near, *parts, other)), jnp.zeros((), F32))
    feature_grad = jnp.swapaxes(total, 1, 2).astype(BF16).reshape(2 * B, B)
    scale = float(node_feats.shape[0] * NZ * NYL * NX) ** (-0.5)
    weight_grad = jnp.where(
        c == 0, jnp.concatenate([w, got]), jnp.concatenate([got, w])
    ) * scale
    return act.reshape(2 * B, B), feature_grad, weight_grad


def solution(mesh):
    placed = (
        P("node", None),
        P(),
        P(("node", "rep"), None),
        P("node", "rep", None, None, None),
        P("node", "rep", None),
        P("node", "rep", None),
        P("node", "rep"),
    )
    return jax.shard_map(
        body,
        mesh=mesh,
        in_specs=placed,
        out_specs=(P(("node", "rep"), None), P(("node", "rep"), None), P()),
        check_vma=False,
    )
```

profile of v0, /device:TPU:0, one launch (start us, length us, event | category | flops | bytes accessed | tf_op | source)
XLA Modules:
  0.0 165.7 jit_solution(12295085598805342459)
XLA Ops:
  0.7 1.2 copy-done
  1.9 1.7 %collective-permute-start.5 = (bf16[2,256,256]{2,1,0:T(8,128)(2,1)S(1)}, bf16[2,256,256]{2,1,0:T(8,128)(2,1)S(1)}, u32[]{:S(2)}, u32[]{:S(2)}) collective-permute-start(bf16[2,256,256]{2,1,0:T(8,128)(2,1)S(1)} %constant_dynamic-slice_fusion), channel_id=1, source_target_pairs={{0,16},{1,17},{2,18},{3,19},{4,20},{5,21},{6,22},{7,23},{8,24},{9,... | collective-permute-start | bytes 786440 | tf_op jit(solution)/shard_map/ppermute | solution.py:51
  3.6 1.5 collective-permute-start
  5.1 1.7 %collective-permute-start.1 = (bf16[2,256,256]{2,1,0:T(8,128)(2,1)S(1)}, bf16[2,256,256]{2,1,0:T(8,128)(2,1)S(1)}, u32[]{:S(2)}, u32[]{:S(2)}) collective-permute-start(bf16[2,256,256]{2,1,0:T(8,128)(2,1)S(1)} %constant_dynamic-slice_fusion), channel_id=1, source_target_pairs={{0,12},{1,97},{2,14},{3,99},{4,0},{5,101},{6,2},{7,103},{8,4},{9,1... | collective-permute-start | bytes 786440 | tf_op jit(solution)/shard_map/ppermute | solution.py:51
  6.9 1.8 %collective-permute-start.2 = (bf16[2,256,256]{2,1,0:T(8,128)(2,1)S(1)}, bf16[2,256,256]{2,1,0:T(8,128)(2,1)S(1)}, u32[]{:S(2)}, u32[]{:S(2)}) collective-permute-start(bf16[2,256,256]{2,1,0:T(8,128)(2,1)S(1)} %constant_dynamic-slice_fusion), channel_id=1, source_target_pairs={{0,8},{1,65},{2,10},{3,67},{4,12},{5,69},{6,14},{7,71},{8,0},{9,73... | collective-permute-start | bytes 786440 | tf_op jit(solution)/shard_map/ppermute | solution.py:51
  8.7 1.3 collective-permute-done.5
  9.9 1.7 collective-permute-start.6
  11.6 1.6 collective-permute-start.7
  13.2 2.0 %collective-permute-start.8 = (bf16[2,256,256]{2,1,0:T(8,128)(2,1)S(1)}, bf16[2,256,256]{2,1,0:T(8,128)(2,1)S(1)}, u32[]{:S(2)}, u32[]{:S(2)}) collective-permute-start(bf16[2,256,256]{2,1,0:T(8,128)(2,1)S(1)} %collective-permute-done.5), channel_id=1, source_target_pairs={{0,8},{1,65},{2,10},{3,67},{4,12},{5,69},{6,14},{7,71},{8,0},{9,73... | collective-permute-start | bytes 786440 | tf_op jit(solution)/shard_map/ppermute | solution.py:51
  15.1 3.2 %collective-permute-start.9 = (bf16[2,256,256]{2,1,0:T(8,128)(2,1)}, bf16[2,256,256]{2,1,0:T(8,128)(2,1)S(1)}, u32[]{:S(2)}, u32[]{:S(2)}) collective-permute-start(bf16[2,256,256]{2,1,0:T(8,128)(2,1)} %bitcast.42), channel_id=1, source_target_pairs={{0,2},{1,3},{2,0},{3,1},{4,6},{5,7},{6,4},{7,5},{8,10},{9,11},{10,... | collective-permute-start | bytes 786440 | tf_op jit(solution)/shard_map/ppermute | solution.py:51
  18.5 2.0 %collective-permute-start.3 = (bf16[8,256,256]{2,1,0:T(8,128)(2,1)S(1)}, bf16[8,256,256]{2,1,0:T(8,128)(2,1)}, u32[]{:S(2)}, u32[]{:S(2)}) collective-permute-start(bf16[8,256,256]{2,1,0:T(8,128)(2,1)S(1)} %pad_maximum_fusion.fa), channel_id=1, source_target_pairs={{0,32},{1,5},{2,34},{3,7},{4,36},{5,9},{6,38},{7,11},{8,40},{9,13}... | collective-permute-start | bytes 3145736 | tf_op jit(solution)/shard_map/ppermute | solution.py:51
  20.5 2.2 %collective-permute-start.4 = (bf16[8,256,256]{2,1,0:T(8,128)(2,1)S(1)}, bf16[8,256,256]{2,1,0:T(8,128)(2,1)}, u32[]{:S(2)}, u32[]{:S(2)}) collective-permute-start(bf16[8,256,256]{2,1,0:T(8,128)(2,1)S(1)} %pad_maximum_fusion.fa), channel_id=1, source_target_pairs={{0,96},{1,13},{2,98},{3,15},{4,100},{5,1},{6,102},{7,3},{8,104},{9... | collective-permute-start | bytes 3145736 | tf_op jit(solution)/shard_map/ppermute | solution.py:51
  22.9 1.2 collective-permute-done.9.cot1
  24.1 1.1 collective-permute-start.11
  25.2 2.1 %collective-permute-start.12 = (bf16[8,256,256]{2,1,0:T(8,128)(2,1)S(1)}, bf16[8,256,256]{2,1,0:T(8,128)(2,1)}, u32[]{:S(2)}, u32[]{:S(2)}) collective-permute-start(bf16[8,256,256]{2,1,0:T(8,128)(2,1)S(1)} %pad_maximum_fusion.1.fb), channel_id=1, source_target_pairs={{0,96},{1,13},{2,98},{3,15},{4,100},{5,1},{6,102},{7,3},{8,104},{9... | collective-permute-start | bytes 3145736 | tf_op jit(solution)/shard_map/ppermute | solution.py:51
  28.5 7.0 %tiles_forward_0.1.refs_0_ = f32[8,256,256]{2,1,0:T(8,128)S(1)} custom-call(s32[160]{0:T(256)S(1)} %select_reduce_fusion.1.tab, s32[9]{0:T(128)S(1)} %convert_reduce_fusion.3.offs, bf16[160,256,256]{2,1,0:T(8,128)(2,1)} %bitcast.44, bf16[8,256,256]{2,1,0:T(8,128)(2,1)S(1)} %pad_maximum_fusion.fa, bf16[8,256,256]{2,1,0:T(8,128)(2,1)S(1)} %pad_maximum_fusion.1.fb), custom_call_target="tpu_custom_call" | custom-call | flops 16777216 | bytes 65536 | tf_op jit(solution)/shard_map/tiles_forward_0/pallas_call | solution.py:174
  35.5 1.8 %collective-permute-start.10 = (bf16[8,256,256]{2,1,0:T(8,128)(2,1)}, bf16[8,256,256]{2,1,0:T(8,128)(2,1)S(1)}, u32[]{:S(2)}, u32[]{:S(2)}) collective-permute-start(bf16[8,256,256]{2,1,0:T(8,128)(2,1)} %collective-permute-done.3.fa), channel_id=1, source_target_pairs={{0,32},{1,5},{2,34},{3,7},{4,36},{5,9},{6,38},{7,11},{8,40},{9,13}... | collective-permute-start | bytes 3145736 | tf_op jit(solution)/shard_map/ppermute | solution.py:51
  37.3 8.3 %tiles_forward_1.1.refs_0_ = f32[8,256,256]{2,1,0:T(8,128)S(1)} custom-call(s32[160]{0:T(256)S(1)} %select_reduce_fusion.1.tab, s32[9]{0:T(128)S(1)} %convert_reduce_fusion.3.offs, bf16[160,256,256]{2,1,0:T(8,128)(2,1)} %bitcast.45, bf16[8,256,256]{2,1,0:T(8,128)(2,1)} %collective-permute-done.3.fa, ...), custom_call_target="tpu_custom_call", output_to_operand_aliasing={{}: (5, {})} | custom-call | flops 16777216 | bytes 65536 | tf_op jit(solution)/shard_map/tiles_forward_1/pallas_call | solution.py:174
  45.6 1.1 collective-permute-done.11.fa
  46.7 3.3 %collective-permute-start.13 = (bf16[8,256,256]{2,1,0:T(8,128)(2,1)}, bf16[8,256,256]{2,1,0:T(8,128)(2,1)S(1)}, u32[]{:S(2)}, u32[]{:S(2)}) collective-permute-start(bf16[8,256,256]{2,1,0:T(8,128)(2,1)} %collective-permute-done.12.fb), channel_id=1, source_target_pairs={{0,96},{1,13},{2,98},{3,15},{4,100},{5,1},{6,102},{7,3},{8,104},{9... | collective-permute-start | bytes 3145736 | tf_op jit(solution)/shard_map/ppermute | solution.py:51
  50.1 6.8 %tiles_forward_2.1.refs_0_ = f32[8,256,256]{2,1,0:T(8,128)S(1)} custom-call(s32[160]{0:T(256)S(1)} %select_reduce_fusion.1.tab, s32[9]{0:T(128)S(1)} %convert_reduce_fusion.3.offs, bf16[160,256,256]{2,1,0:T(8,128)(2,1)} %bitcast.46, bf16[8,256,256]{2,1,0:T(8,128)(2,1)} %collective-permute-done.11.fa, ...), custom_call_target="tpu_custom_call", output_to_operand_aliasing={{}: (5, {})} | custom-call | flops 16777216 | bytes 65536 | tf_op jit(solution)/shard_map/tiles_forward_2/pallas_call | solution.py:174
  56.9 1.0 collective-permute-done.10.fa
  57.9 4.8 %collective-permute-done.13.fb = bf16[8,256,256]{2,1,0:T(8,128)(2,1)S(1)} collective-permute-done((bf16[8,256,256]{2,1,0:T(8,128)(2,1)}, bf16[8,256,256]{2,1,0:T(8,128)(2,1)S(1)}, u32[]{:S(2)}, u32[]{:S(2)}) %collective-permute-start.13) | collective-permute-done | bytes 1048608 | tf_op jit(solution)/shard_map/ppermute | solution.py:51
  62.7 6.0 %tiles_forward_3.1 = f32[8,256,256]{2,1,0:T(8,128)S(1)} custom-call(s32[160]{0:T(256)S(1)} %select_reduce_fusion.1.tab, s32[9]{0:T(128)S(1)} %convert_reduce_fusion.3.offs, bf16[160,256,256]{2,1,0:T(8,128)(2,1)} %bitcast.47, bf16[8,256,256]{2,1,0:T(8,128)(2,1)S(1)} %collective-permute-done.10.fa, ...), custom_call_target="tpu_custom_call", output_to_operand_aliasing={{}: (5, {})} | custom-call | flops 16777216 | bytes 65536 | tf_op jit(solution)/shard_map/tiles_forward_3/pallas_call | solution.py:174
  69.0 2.6 %collective-permute-done.14 = f32[4,256,256]{2,1,0:T(8,128)S(1)} collective-permute-done((f32[4,256,256]{2,1,0:T(8,128)S(1)}, f32[4,256,256]{2,1,0:T(8,128)S(1)}, u32[]{:S(2)}, u32[]{:S(2)}) %collective-permute-start.14) | collective-permute-done | bytes 1048608 | tf_op jit(solution)/shard_map/ppermute | solution.py:51
  71.8 2.8 %collective-permute-start.15 = (bf16[4,256,256]{2,1,0:T(8,128)(2,1)S(1)}, bf16[4,256,256]{2,1,0:T(8,128)(2,1)S(1)}, u32[]{:S(2)}, u32[]{:S(2)}) collective-permute-start(bf16[4,256,256]{2,1,0:T(8,128)(2,1)S(1)} %fusion.near), channel_id=1, source_target_pairs={{0,2},{1,3},{2,0},{3,1},{4,6},{5,7},{6,4},{7,5},{8,10},{9,11},{10,... | collective-permute-start | bytes 1572872 | tf_op jit(solution)/shard_map/ppermute | solution.py:51
  74.8 12.6 %collective-permute-done.15.far = bf16[4,256,256]{2,1,0:T(8,128)(2,1)S(1)} collective-permute-done((bf16[4,256,256]{2,1,0:T(8,128)(2,1)S(1)}, bf16[4,256,256]{2,1,0:T(8,128)(2,1)S(1)}, u32[]{:S(2)}, u32[]{:S(2)}) %collective-permute-start.15) | collective-permute-done | bytes 524320 | tf_op jit(solution)/shard_map/ppermute | solution.py:51
  87.4 1.4 dense.1
  89.7 1.2 collective-permute-done.17
  90.9 5.0 %tiles_backward_3.1 = (bf16[8,256,256]{2,1,0:T(8,128)(2,1)S(1)}, bf16[8,256,256]{2,1,0:T(8,128)(2,1)S(1)}) custom-call(s32[160]{0:T(256)S(1)} %select_reduce_fusion.tab, s32[9]{0:T(128)S(1)} %convert_reduce_fusion.2.offs, bf16[160,256,256]{2,1,0:T(8,128)(2,1)} %bitcast.48, bf16[4,256,256]{2,1,0:T(8,128)(2,1)S(1)} %get-tuple-element.68.d0, ...), custom_call_target="tpu_custom_call" | custom-call | flops 16777216 | bytes 65536 | tf_op jit(solution)/shard_map/tiles_backward_3/pallas_call | solution.py:223
  96.2 6.5 %collective-permute-start.23 = (bf16[8,256,256]{2,1,0:T(8,128)(2,1)S(1)}, bf16[8,256,256]{2,1,0:T(8,128)(2,1)S(1)}, u32[]{:S(2)}, u32[]{:S(2)}) collective-permute-start(bf16[8,256,256]{2,1,0:T(8,128)(2,1)S(1)} %get-tuple-element.54), channel_id=1, source_target_pairs={{0,96},{1,13},{2,98},{3,15},{4,100},{5,1},{6,102},{7,3},{8,104},{9... | collective-permute-start | bytes 3145736 | tf_op jit(solution)/shard_map/ppermute | solution.py:51
  102.8 5.9 %tiles_backward_0.1 = (bf16[8,256,256]{2,1,0:T(8,128)(2,1)S(1)}, bf16[8,256,256]{2,1,0:T(8,128)(2,1)S(1)}) custom-call(s32[160]{0:T(256)S(1)} %select_reduce_fusion.tab, s32[9]{0:T(128)S(1)} %convert_reduce_fusion.2.offs, bf16[160,256,256]{2,1,0:T(8,128)(2,1)} %bitcast.49, bf16[4,256,256]{2,1,0:T(8,128)(2,1)S(1)} %get-tuple-element.68.d0, ...), custom_call_target="tpu_custom_call" | custom-call | flops 16777216 | bytes 65536 | tf_op jit(solution)/shard_map/tiles_backward_0/pallas_call | solution.py:223
  108.8 6.1 %tiles_backward_1.1 = (bf16[2176,256]{1,0:T(8,128)(2,1)S(1)}, bf16[2176,256]{1,0:T(8,128)(2,1)S(1)}) custom-call(s32[160]{0:T(256)S(1)} %select_reduce_fusion.tab, s32[9]{0:T(128)S(1)} %convert_reduce_fusion.2.offs, bf16[160,256,256]{2,1,0:T(8,128)(2,1)} %bitcast.50, bf16[4,256,256]{2,1,0:T(8,128)(2,1)S(1)} %get-tuple-element.68.d0, ...), custom_call_target="tpu_custom_call" | custom-call | flops 16777216 | bytes 65536 | tf_op jit(solution)/shard_map/tiles_backward_1/pallas_call | solution.py:223
  114.8 0.9 collective-permute-start.19
  115.8 1.2 collective-permute-start.20
  117.0 4.9 %tiles_backward_2.1 = (bf16[8,256,256]{2,1,0:T(8,128)(2,1)S(1)}, bf16[8,256,256]{2,1,0:T(8,128)(2,1)S(1)}) custom-call(s32[160]{0:T(256)S(1)} %select_reduce_fusion.tab, s32[9]{0:T(128)S(1)} %convert_reduce_fusion.2.offs, bf16[160,256,256]{2,1,0:T(8,128)(2,1)} %bitcast.51, bf16[4,256,256]{2,1,0:T(8,128)(2,1)S(1)} %get-tuple-element.68.d0, ...), custom_call_target="tpu_custom_call" | custom-call | flops 16777216 | bytes 65536 | tf_op jit(solution)/shard_map/tiles_backward_2/pallas_call | solution.py:223
  121.8 3.2 %collective-permute-start.28 = (bf16[8,256,256]{2,1,0:T(8,128)(2,1)S(1)}, bf16[8,256,256]{2,1,0:T(8,128)(2,1)S(1)}, u32[]{:S(2)}, u32[]{:S(2)}) collective-permute-start(bf16[8,256,256]{2,1,0:T(8,128)(2,1)S(1)} %get-tuple-element.75), channel_id=1, source_target_pairs={{0,96},{1,13},{2,98},{3,15},{4,100},{5,1},{6,102},{7,3},{8,104},{9... | collective-permute-start | bytes 3145736 | tf_op jit(solution)/shard_map/ppermute | solution.py:51
  125.1 0.9 collective-permute-start.24
  126.0 5.6 %collective-permute-done.21 = bf16[128,256]{1,0:T(8,128)(2,1)S(1)} collective-permute-done((bf16[128,256]{1,0:T(8,128)(2,1)S(1)}, bf16[128,256]{1,0:T(8,128)(2,1)S(1)}, u32[]{:S(2)}, u32[]{:S(2)}) %collective-permute-start.21) | collective-permute-done | bytes 65568 | tf_op jit(solution)/shard_map/ppermute | solution.py:51
  131.6 1.6 collective-permute-done.20
  133.3 8.3 %collective-permute-done.28 = bf16[8,256,256]{2,1,0:T(8,128)(2,1)S(1)} collective-permute-done((bf16[8,256,256]{2,1,0:T(8,128)(2,1)S(1)}, bf16[8,256,256]{2,1,0:T(8,128)(2,1)S(1)}, u32[]{:S(2)}, u32[]{:S(2)}) %collective-permute-start.28) | collective-permute-done | bytes 1048608 | tf_op jit(solution)/shard_map/ppermute | solution.py:51
  142.2 3.2 %collective-permute-start.31 = (bf16[640,256]{1,0:T(8,128)(2,1)S(1)}, bf16[640,256]{1,0:T(8,128)(2,1)S(1)}, u32[]{:S(2)}, u32[]{:S(2)}) collective-permute-start(bf16[640,256]{1,0:T(8,128)(2,1)S(1)} %get-tuple-element.103), channel_id=1, source_target_pairs={{0,12},{1,97},{2,14},{3,99},{4,0},{5,101},{6,2},{7,103},{8,4},{9,1... | collective-permute-start | bytes 983048 | tf_op jit(solution)/shard_map/ppermute | solution.py:51
  145.5 8.2 %collective-permute-done.24 = bf16[8,256,256]{2,1,0:T(8,128)(2,1)S(1)} collective-permute-done((bf16[8,256,256]{2,1,0:T(8,128)(2,1)S(1)}, bf16[8,256,256]{2,1,0:T(8,128)(2,1)S(1)}, u32[]{:S(2)}, u32[]{:S(2)}) %collective-permute-start.24) | collective-permute-done | bytes 1048608 | tf_op jit(solution)/shard_map/ppermute | solution.py:51
  154.3 3.2 %collective-permute-start.27 = (bf16[2,256,256]{2,1,0:T(8,128)(2,1)S(1)}, bf16[2,256,256]{2,1,0:T(8,128)(2,1)S(1)}, u32[]{:S(2)}, u32[]{:S(2)}) collective-permute-start(bf16[2,256,256]{2,1,0:T(8,128)(2,1)S(1)} %get-tuple-element.88), channel_id=1, source_target_pairs={{0,12},{1,97},{2,14},{3,99},{4,0},{5,101},{6,2},{7,103},{8,4},{9,1... | collective-permute-start | bytes 786440 | tf_op jit(solution)/shard_map/ppermute | solution.py:51
  158.0 1.3 collective-permute-done.33
  160.1 2.0 %collective-permute-done.25 = bf16[2,256,256]{2,1,0:T(8,128)(2,1)S(1)} collective-permute-done((bf16[2,256,256]{2,1,0:T(8,128)(2,1)S(1)}, bf16[2,256,256]{2,1,0:T(8,128)(2,1)S(1)}, u32[]{:S(2)}, u32[]{:S(2)}) %collective-permute-start.25) | collective-permute-done | bytes 262176 | tf_op jit(solution)/shard_map/ppermute | solution.py:51
  162.2 2.5 %collective-permute-done.26 = bf16[2,256,256]{2,1,0:T(8,128)(2,1)S(1)} collective-permute-done((bf16[2,256,256]{2,1,0:T(8,128)(2,1)S(1)}, bf16[2,256,256]{2,1,0:T(8,128)(2,1)S(1)}, u32[]{:S(2)}, u32[]{:S(2)}) %collective-permute-start.26) | collective-permute-done | bytes 262176 | tf_op jit(solution)/shard_map/ppermute | solution.py:51
  164.9 0.8 copy.14
  (71 shorter events, 5.5 us)
Async XLA Ops:
  0.6 1.2 copy-start
  1.9 8.0 %collective-permute-start.5 = (bf16[2,256,256]{2,1,0:T(8,128)(2,1)S(1)}, bf16[2,256,256]{2,1,0:T(8,128)(2,1)S(1)}, u32[]{:S(2)}, u32[]{:S(2)}) collective-permute-start(bf16[2,256,256]{2,1,0:T(8,128)(2,1)S(1)} %constant_dynamic-slice_fusion), channel_id=1, source_target_pairs={{0,16},{1,17},{2,18},{3,19},{4,20},{5,21},{6,22},{7,23},{8,24},{9,... | collective-permute-start | bytes 786440 | tf_op jit(solution)/shard_map/ppermute | solution.py:51
  3.6 9.5 %collective-permute-start = (bf16[2,256,256]{2,1,0:T(8,128)(2,1)S(1)}, bf16[2,256,256]{2,1,0:T(8,128)(2,1)S(1)}, u32[]{:S(2)}, u32[]{:S(2)}) collective-permute-start(bf16[2,256,256]{2,1,0:T(8,128)(2,1)S(1)} %constant_dynamic-slice_fusion), channel_id=1, source_target_pairs={{0,4},{1,33},{2,6},{3,35},{4,8},{5,37},{6,10},{7,39},{8,12},{9,41}... | collective-permute-start | bytes 786440 | tf_op jit(solution)/shard_map/ppermute | solution.py:51
  5.1 10.0 %collective-permute-start.1 = (bf16[2,256,256]{2,1,0:T(8,128)(2,1)S(1)}, bf16[2,256,256]{2,1,0:T(8,128)(2,1)S(1)}, u32[]{:S(2)}, u32[]{:S(2)}) collective-permute-start(bf16[2,256,256]{2,1,0:T(8,128)(2,1)S(1)} %constant_dynamic-slice_fusion), channel_id=1, source_target_pairs={{0,12},{1,97},{2,14},{3,99},{4,0},{5,101},{6,2},{7,103},{8,4},{9,1... | collective-permute-start | bytes 786440 | tf_op jit(solution)/shard_map/ppermute | solution.py:51
  6.9 11.5 %collective-permute-start.2 = (bf16[2,256,256]{2,1,0:T(8,128)(2,1)S(1)}, bf16[2,256,256]{2,1,0:T(8,128)(2,1)S(1)}, u32[]{:S(2)}, u32[]{:S(2)}) collective-permute-start(bf16[2,256,256]{2,1,0:T(8,128)(2,1)S(1)} %constant_dynamic-slice_fusion), channel_id=1, source_target_pairs={{0,8},{1,65},{2,10},{3,67},{4,12},{5,69},{6,14},{7,71},{8,0},{9,73... | collective-permute-start | bytes 786440 | tf_op jit(solution)/shard_map/ppermute | solution.py:51
  9.9 10.6 %collective-permute-start.6 = (bf16[2,256,256]{2,1,0:T(8,128)(2,1)S(1)}, bf16[2,256,256]{2,1,0:T(8,128)(2,1)S(1)}, u32[]{:S(2)}, u32[]{:S(2)}) collective-permute-start(bf16[2,256,256]{2,1,0:T(8,128)(2,1)S(1)} %collective-permute-done.5), channel_id=1, source_target_pairs={{0,4},{1,33},{2,6},{3,35},{4,8},{5,37},{6,10},{7,39},{8,12},{9,41}... | collective-permute-start | bytes 786440 | tf_op jit(solution)/shard_map/ppermute | solution.py:51
  11.6 11.1 %collective-permute-start.7 = (bf16[2,256,256]{2,1,0:T(8,128)(2,1)S(1)}, bf16[2,256,256]{2,1,0:T(8,128)(2,1)S(1)}, u32[]{:S(2)}, u32[]{:S(2)}) collective-permute-start(bf16[2,256,256]{2,1,0:T(8,128)(2,1)S(1)} %collective-permute-done.5), channel_id=1, source_target_pairs={{0,12},{1,97},{2,14},{3,99},{4,0},{5,101},{6,2},{7,103},{8,4},{9,1... | collective-permute-start | bytes 786440 | tf_op jit(solution)/shard_map/ppermute | solution.py:51
  13.2 9.5 %collective-permute-start.8 = (bf16[2,256,256]{2,1,0:T(8,128)(2,1)S(1)}, bf16[2,256,256]{2,1,0:T(8,128)(2,1)S(1)}, u32[]{:S(2)}, u32[]{:S(2)}) collective-permute-start(bf16[2,256,256]{2,1,0:T(8,128)(2,1)S(1)} %collective-permute-done.5), channel_id=1, source_target_pairs={{0,8},{1,65},{2,10},{3,67},{4,12},{5,69},{6,14},{7,71},{8,0},{9,73... | collective-permute-start | bytes 786440 | tf_op jit(solution)/shard_map/ppermute | solution.py:51
  15.1 8.9 %collective-permute-start.9 = (bf16[2,256,256]{2,1,0:T(8,128)(2,1)}, bf16[2,256,256]{2,1,0:T(8,128)(2,1)S(1)}, u32[]{:S(2)}, u32[]{:S(2)}) collective-permute-start(bf16[2,256,256]{2,1,0:T(8,128)(2,1)} %bitcast.42), channel_id=1, source_target_pairs={{0,2},{1,3},{2,0},{3,1},{4,6},{5,7},{6,4},{7,5},{8,10},{9,11},{10,... | collective-permute-start | bytes 786440 | tf_op jit(solution)/shard_map/ppermute | solution.py:51
  18.5 9.5 %copy-start.3 = (s32[1,1,160]{2,1,0:T(1,128)S(1)}, s32[1,1,160]{2,1,0:T(1,128)}, u32[]{:S(2)}) copy-start(s32[1,1,160]{2,1,0:T(1,128)} %param.12) | copy-start | bytes 1924
  18.5 9.5 %copy-start.4 = (s32[1,1,160]{2,1,0:T(1,128)S(1)}, s32[1,1,160]{2,1,0:T(1,128)}, u32[]{:S(2)}) copy-start(s32[1,1,160]{2,1,0:T(1,128)} %param.11) | copy-start | bytes 1924
  18.5 17.0 %collective-permute-start.3 = (bf16[8,256,256]{2,1,0:T(8,128)(2,1)S(1)}, bf16[8,256,256]{2,1,0:T(8,128)(2,1)}, u32[]{:S(2)}, u32[]{:S(2)}) collective-permute-start(bf16[8,256,256]{2,1,0:T(8,128)(2,1)S(1)} %pad_maximum_fusion.fa), channel_id=1, source_target_pairs={{0,32},{1,5},{2,34},{3,7},{4,36},{5,9},{6,38},{7,11},{8,40},{9,13}... | collective-permute-start | bytes 3145736 | tf_op jit(solution)/shard_map/ppermute | solution.py:51
  20.5 15.0 %collective-permute-start.4 = (bf16[8,256,256]{2,1,0:T(8,128)(2,1)S(1)}, bf16[8,256,256]{2,1,0:T(8,128)(2,1)}, u32[]{:S(2)}, u32[]{:S(2)}) collective-permute-start(bf16[8,256,256]{2,1,0:T(8,128)(2,1)S(1)} %pad_maximum_fusion.fa), channel_id=1, source_target_pairs={{0,96},{1,13},{2,98},{3,15},{4,100},{5,1},{6,102},{7,3},{8,104},{9... | collective-permute-start | bytes 3145736 | tf_op jit(solution)/shard_map/ppermute | solution.py:51
  24.1 22.7 %collective-permute-start.11 = (bf16[8,256,256]{2,1,0:T(8,128)(2,1)S(1)}, bf16[8,256,256]{2,1,0:T(8,128)(2,1)}, u32[]{:S(2)}, u32[]{:S(2)}) collective-permute-start(bf16[8,256,256]{2,1,0:T(8,128)(2,1)S(1)} %pad_maximum_fusion.1.fb), channel_id=1, source_target_pairs={{0,32},{1,5},{2,34},{3,7},{4,36},{5,9},{6,38},{7,11},{8,40},{9,13}... | collective-permute-start | bytes 3145736 | tf_op jit(solution)/shard_map/ppermute | solution.py:51
  25.2 21.6 %collective-permute-start.12 = (bf16[8,256,256]{2,1,0:T(8,128)(2,1)S(1)}, bf16[8,256,256]{2,1,0:T(8,128)(2,1)}, u32[]{:S(2)}, u32[]{:S(2)}) collective-permute-start(bf16[8,256,256]{2,1,0:T(8,128)(2,1)S(1)} %pad_maximum_fusion.1.fb), channel_id=1, source_target_pairs={{0,96},{1,13},{2,98},{3,15},{4,100},{5,1},{6,102},{7,3},{8,104},{9... | collective-permute-start | bytes 3145736 | tf_op jit(solution)/shard_map/ppermute | solution.py:51
  35.5 22.3 %collective-permute-start.10 = (bf16[8,256,256]{2,1,0:T(8,128)(2,1)}, bf16[8,256,256]{2,1,0:T(8,128)(2,1)S(1)}, u32[]{:S(2)}, u32[]{:S(2)}) collective-permute-start(bf16[8,256,256]{2,1,0:T(8,128)(2,1)} %collective-permute-done.3.fa), channel_id=1, source_target_pairs={{0,32},{1,5},{2,34},{3,7},{4,36},{5,9},{6,38},{7,11},{8,40},{9,13}... | collective-permute-start | bytes 3145736 | tf_op jit(solution)/shard_map/ppermute | solution.py:51
  46.7 16.0 %collective-permute-start.13 = (bf16[8,256,256]{2,1,0:T(8,128)(2,1)}, bf16[8,256,256]{2,1,0:T(8,128)(2,1)S(1)}, u32[]{:S(2)}, u32[]{:S(2)}) collective-permute-start(bf16[8,256,256]{2,1,0:T(8,128)(2,1)} %collective-permute-done.12.fb), channel_id=1, source_target_pairs={{0,96},{1,13},{2,98},{3,15},{4,100},{5,1},{6,102},{7,3},{8,104},{9... | collective-permute-start | bytes 3145736 | tf_op jit(solution)/shard_map/ppermute | solution.py:51
  68.8 18.6 %copy-start.1 = (bf16[512,256]{1,0:T(8,128)(2,1)S(1)}, bf16[512,256]{1,0:T(8,128)(2,1)}, u32[]{:S(2)}) copy-start(bf16[512,256]{1,0:T(8,128)(2,1)} %param.9) | copy-start | bytes 786436
  68.8 18.5 %copy-start.2 = (bf16[256,256]{1,0:T(8,128)(2,1)S(1)}, bf16[256,256]{1,0:T(8,128)(2,1)}, u32[]{:S(2)}) copy-start(bf16[256,256]{1,0:T(8,128)(2,1)} %w_ref.1) | copy-start | bytes 393220
  68.9 2.7 %collective-permute-start.14 = (f32[4,256,256]{2,1,0:T(8,128)S(1)}, f32[4,256,256]{2,1,0:T(8,128)S(1)}, u32[]{:S(2)}, u32[]{:S(2)}) collective-permute-start(f32[4,256,256]{2,1,0:T(8,128)S(1)} %slice.163), channel_id=1, source_target_pairs={{0,1},{1,0},{2,3},{3,2},{4,5},{5,4},{6,7},{7,6},{8,9},{9,8},{10,11... | collective-permute-start | bytes 3145736 | tf_op jit(solution)/shard_map/ppermute | solution.py:51
  71.8 15.5 %collective-permute-start.15 = (bf16[4,256,256]{2,1,0:T(8,128)(2,1)S(1)}, bf16[4,256,256]{2,1,0:T(8,128)(2,1)S(1)}, u32[]{:S(2)}, u32[]{:S(2)}) collective-permute-start(bf16[4,256,256]{2,1,0:T(8,128)(2,1)S(1)} %fusion.near), channel_id=1, source_target_pairs={{0,2},{1,3},{2,0},{3,1},{4,6},{5,7},{6,4},{7,5},{8,10},{9,11},{10,... | collective-permute-start | bytes 1572872 | tf_op jit(solution)/shard_map/ppermute | solution.py:51
  88.8 2.1 %collective-permute-start.16 = (bf16[4,256,256]{2,1,0:T(8,128)(2,1)S(1)}, bf16[4,256,256]{2,1,0:T(8,128)(2,1)S(1)}, u32[]{:S(2)}, u32[]{:S(2)}) collective-permute-start(bf16[4,256,256]{2,1,0:T(8,128)(2,1)S(1)} %get-tuple-element.68.d0), channel_id=1, source_target_pairs={{0,1},{1,0},{2,3},{3,2},{4,5},{5,4},{6,7},{7,6},{8,9},{9,8},{10,11... | collective-permute-start | bytes 1572872 | tf_op jit(solution)/shard_map/ppermute | solution.py:51
  88.8 2.0 %collective-permute-start.17 = (f32[128,256]{1,0:T(8,128)S(1)}, f32[128,256]{1,0:T(8,128)S(1)}, u32[]{:S(2)}, u32[]{:S(2)}) collective-permute-start(f32[128,256]{1,0:T(8,128)S(1)} %dynamic-slice_bitcast_fusion), channel_id=1, source_target_pairs={{0,1},{1,0},{2,3},{3,2},{4,5},{5,4},{6,7},{7,6},{8,9},{9,8},{10,11... | collective-permute-start | bytes 393224 | tf_op jit(solution)/shard_map/ppermute | solution.py:51
  95.9 21.1 %collective-permute-start.22 = (bf16[8,256,256]{2,1,0:T(8,128)(2,1)S(1)}, bf16[8,256,256]{2,1,0:T(8,128)(2,1)S(1)}, u32[]{:S(2)}, u32[]{:S(2)}) collective-permute-start(bf16[8,256,256]{2,1,0:T(8,128)(2,1)S(1)} %get-tuple-element.53), channel_id=1, source_target_pairs={{0,32},{1,5},{2,34},{3,7},{4,36},{5,9},{6,38},{7,11},{8,40},{9,13}... | collective-permute-start | bytes 3145736 | tf_op jit(solution)/shard_map/ppermute | solution.py:51
  96.2 20.7 %collective-permute-start.23 = (bf16[8,256,256]{2,1,0:T(8,128)(2,1)S(1)}, bf16[8,256,256]{2,1,0:T(8,128)(2,1)S(1)}, u32[]{:S(2)}, u32[]{:S(2)}) collective-permute-start(bf16[8,256,256]{2,1,0:T(8,128)(2,1)S(1)} %get-tuple-element.54), channel_id=1, source_target_pairs={{0,96},{1,13},{2,98},{3,15},{4,100},{5,1},{6,102},{7,3},{8,104},{9... | collective-permute-start | bytes 3145736 | tf_op jit(solution)/shard_map/ppermute | solution.py:51
  102.7 6.0 %collective-permute-start.18 = (f32[128,256]{1,0:T(8,128)S(1)}, f32[128,256]{1,0:T(8,128)S(1)}, u32[]{:S(2)}, u32[]{:S(2)}) collective-permute-start(f32[128,256]{1,0:T(8,128)S(1)} %bitcast_add_fusion), channel_id=1, source_target_pairs={{0,16},{1,17},{2,18},{3,19},{4,20},{5,21},{6,22},{7,23},{8,24},{9,... | collective-permute-start | bytes 393224 | tf_op jit(solution)/shard_map/ppermute | solution.py:51
  114.8 16.8 %collective-permute-start.19 = (bf16[2176,256]{1,0:T(8,128)(2,1)S(1)}, bf16[2176,256]{1,0:T(8,128)(2,1)S(1)}, u32[]{:S(2)}, u32[]{:S(2)}) collective-permute-start(bf16[2176,256]{1,0:T(8,128)(2,1)S(1)} %get-tuple-element.65), channel_id=1, source_target_pairs={{0,96},{1,13},{2,98},{3,15},{4,100},{5,1},{6,102},{7,3},{8,104},{9... | collective-permute-start | bytes 3342344 | tf_op jit(solution)/shard_map/ppermute | solution.py:51
  115.8 17.4 %collective-permute-start.20 = (bf16[2176,256]{1,0:T(8,128)(2,1)S(1)}, bf16[2176,256]{1,0:T(8,128)(2,1)S(1)}, u32[]{:S(2)}, u32[]{:S(2)}) collective-permute-start(bf16[2176,256]{1,0:T(8,128)(2,1)S(1)} %get-tuple-element.66), channel_id=1, source_target_pairs={{0,32},{1,5},{2,34},{3,7},{4,36},{5,9},{6,38},{7,11},{8,40},{9,13}... | collective-permute-start | bytes 3342344 | tf_op jit(solution)/shard_map/ppermute | solution.py:51
  121.8 19.8 %collective-permute-start.28 = (bf16[8,256,256]{2,1,0:T(8,128)(2,1)S(1)}, bf16[8,256,256]{2,1,0:T(8,128)(2,1)S(1)}, u32[]{:S(2)}, u32[]{:S(2)}) collective-permute-start(bf16[8,256,256]{2,1,0:T(8,128)(2,1)S(1)} %get-tuple-element.75), channel_id=1, source_target_pairs={{0,96},{1,13},{2,98},{3,15},{4,100},{5,1},{6,102},{7,3},{8,104},{9... | collective-permute-start | bytes 3145736 | tf_op jit(solution)/shard_map/ppermute | solution.py:51
  125.1 6.5 %collective-permute-start.21 = (bf16[128,256]{1,0:T(8,128)(2,1)S(1)}, bf16[128,256]{1,0:T(8,128)(2,1)S(1)}, u32[]{:S(2)}, u32[]{:S(2)}) collective-permute-start(bf16[128,256]{1,0:T(8,128)(2,1)S(1)} %add_convert_fusion.2.refs_0_), channel_id=1, source_target_pairs={{0,64},{1,9},{2,66},{3,11},{4,68},{5,13},{6,70},{7,15},{8,72},{9,1... | collective-permute-start | bytes 196616 | tf_op jit(solution)/shard_map/ppermute | solution.py:51
  125.1 28.7 %collective-permute-start.24 = (bf16[8,256,256]{2,1,0:T(8,128)(2,1)S(1)}, bf16[8,256,256]{2,1,0:T(8,128)(2,1)S(1)}, u32[]{:S(2)}, u32[]{:S(2)}) collective-permute-start(bf16[8,256,256]{2,1,0:T(8,128)(2,1)S(1)} %get-tuple-element.72), channel_id=1, source_target_pairs={{0,32},{1,5},{2,34},{3,7},{4,36},{5,9},{6,38},{7,11},{8,40},{9,13}... | collective-permute-start | bytes 3145736 | tf_op jit(solution)/shard_map/ppermute | solution.py:51
  142.1 12.2 %collective-permute-start.29 = (bf16[640,256]{1,0:T(8,128)(2,1)S(1)}, bf16[640,256]{1,0:T(8,128)(2,1)S(1)}, u32[]{:S(2)}, u32[]{:S(2)}) collective-permute-start(bf16[640,256]{1,0:T(8,128)(2,1)S(1)} %get-tuple-element.101), channel_id=1, source_target_pairs={{0,8},{1,65},{2,10},{3,67},{4,12},{5,69},{6,14},{7,71},{8,0},{9,73... | collective-permute-start | bytes 983048 | tf_op jit(solution)/shard_map/ppermute | solution.py:51
  142.2 15.4 %collective-permute-start.30 = (bf16[640,256]{1,0:T(8,128)(2,1)S(1)}, bf16[640,256]{1,0:T(8,128)(2,1)S(1)}, u32[]{:S(2)}, u32[]{:S(2)}) collective-permute-start(bf16[640,256]{1,0:T(8,128)(2,1)S(1)} %get-tuple-element.102), channel_id=1, source_target_pairs={{0,4},{1,33},{2,6},{3,35},{4,8},{5,37},{6,10},{7,39},{8,12},{9,41}... | collective-permute-start | bytes 983048 | tf_op jit(solution)/shard_map/ppermute | solution.py:51
  142.2 15.3 %collective-permute-start.31 = (bf16[640,256]{1,0:T(8,128)(2,1)S(1)}, bf16[640,256]{1,0:T(8,128)(2,1)S(1)}, u32[]{:S(2)}, u32[]{:S(2)}) collective-permute-start(bf16[640,256]{1,0:T(8,128)(2,1)S(1)} %get-tuple-element.103), channel_id=1, source_target_pairs={{0,12},{1,97},{2,14},{3,99},{4,0},{5,101},{6,2},{7,103},{8,4},{9,1... | collective-permute-start | bytes 983048 | tf_op jit(solution)/shard_map/ppermute | solution.py:51
  154.1 8.1 %collective-permute-start.25 = (bf16[2,256,256]{2,1,0:T(8,128)(2,1)S(1)}, bf16[2,256,256]{2,1,0:T(8,128)(2,1)S(1)}, u32[]{:S(2)}, u32[]{:S(2)}) collective-permute-start(bf16[2,256,256]{2,1,0:T(8,128)(2,1)S(1)} %get-tuple-element.87), channel_id=1, source_target_pairs={{0,8},{1,65},{2,10},{3,67},{4,12},{5,69},{6,14},{7,71},{8,0},{9,73... | collective-permute-start | bytes 786440 | tf_op jit(solution)/shard_map/ppermute | solution.py:51
  154.2 10.5 %collective-permute-start.26 = (bf16[2,256,256]{2,1,0:T(8,128)(2,1)S(1)}, bf16[2,256,256]{2,1,0:T(8,128)(2,1)S(1)}, u32[]{:S(2)}, u32[]{:S(2)}) collective-permute-start(bf16[2,256,256]{2,1,0:T(8,128)(2,1)S(1)} %get-tuple-element.89), channel_id=1, source_target_pairs={{0,4},{1,33},{2,6},{3,35},{4,8},{5,37},{6,10},{7,39},{8,12},{9,41}... | collective-permute-start | bytes 786440 | tf_op jit(solution)/shard_map/ppermute | solution.py:51
  154.3 10.4 %collective-permute-start.27 = (bf16[2,256,256]{2,1,0:T(8,128)(2,1)S(1)}, bf16[2,256,256]{2,1,0:T(8,128)(2,1)S(1)}, u32[]{:S(2)}, u32[]{:S(2)}) collective-permute-start(bf16[2,256,256]{2,1,0:T(8,128)(2,1)S(1)} %get-tuple-element.88), channel_id=1, source_target_pairs={{0,12},{1,97},{2,14},{3,99},{4,0},{5,101},{6,2},{7,103},{8,4},{9,1... | collective-permute-start | bytes 786440 | tf_op jit(solution)/shard_map/ppermute | solution.py:51
  157.8 6.8 %collective-permute-start.32 = (bf16[2,256,256]{2,1,0:T(8,128)(2,1)S(1)}, bf16[2,256,256]{2,1,0:T(8,128)(2,1)S(1)}, u32[]{:S(2)}, u32[]{:S(2)}) collective-permute-start(bf16[2,256,256]{2,1,0:T(8,128)(2,1)S(1)} %fusion.1), channel_id=1, source_target_pairs={{0,16},{1,17},{2,18},{3,19},{4,20},{5,21},{6,22},{7,23},{8,24},{9,... | collective-permute-start | bytes 786440 | tf_op jit(solution)/shard_map/ppermute | solution.py:51
  157.9 1.4 collective-permute-start.33
where the time goes:
time: 168 us; the launch traced here: 166 us
  waiting for transfers between devices  55.5 us (33%)
  Pallas kernels  51.4 us (31%)
  starting transfers between devices  51.3 us (31%)
  other arithmetic  3.52 us (2%)
  local copies, waits for them, and re-layouts  2.39 us (1%)
  between operations  1.69 us (1%)
    ppermute x34, waiting for transfers between devices, send(): return lax.ppermute(value, AXES, pairs)  55.5 us
    ppermute x34, starting transfers between devices, send(): return lax.ppermute(value, AXES, pairs)  51.3 us
    pallas_call x4, Pallas kernels, forward(): pl.pallas_call(functools.partial(_forward_kernel, chunk), name=f'tiles_fo...  28.1 us
    pallas_call x4, Pallas kernels, backward(): pl.pallas_call(functools.partial(_backward_kernel, chunk, len(adds)), nam...  21.9 us
  transfers between devices with their start and end apart: 34, of which 15 were waited for; matrix products, arithmetic and copies ran while one was open for 2% of the time, Pallas kernels for 24%

commit v1 on v0

--- a/solution.py
+++ b/solution.py
@@ -333,21 +333,19 @@
     keep = lax.dynamic_slice_in_dim(whole, c * half, half, 0)
     give = lax.dynamic_slice_in_dim(whole, (1 - c) * half, half, 0)
     d1, got = lax.optimization_barrier((send(d0, CC), send(give, CC)))
-    w = keep + got
+    w = (keep + got).astype(BF16)
 
     fa, fb = backward(3, bwd, boffs, tiles, d0, d1)
     ra, rb = send(fa, VP), send(fb, VM)
     d0, d1, fa, fb, w = lax.optimization_barrier((d0, d1, fa, fb, w))
-    w1 = send(w, YN)
-    lo, hi = backward(0, bwd, boffs, tiles, d0, d1)
-    d0, d1, lo, hi, w1 = lax.optimization_barrier((d0, d1, lo, hi, w1))
-    w = (w + w1).astype(BF16)
     w2 = send(w, V2)
     m1, p1 = backward(1, bwd, boffs, tiles, d0, d1, (w,))
     s_hi, s_lo = send(p1, VP), send(m1, VM)
     d0, d1, m1, p1, ra, rb = lax.optimization_barrier((d0, d1, m1, p1, ra, rb))
     m2, p2 = backward(2, bwd, boffs, tiles, d0, d1, (rb, ra))
     t_lo, t_hi = send(p2, VP), send(m2, VM)
+    d0, d1, m2, p2 = lax.optimization_barrier((d0, d1, m2, p2))
+    lo, hi = backward(0, bwd, boffs, tiles, d0, d1)
     s_lo, s_hi, w2 = lax.optimization_barrier((s_lo, s_hi, w2))
     w = ring_sum(w, w2, s_hi[8 * B :], s_lo[8 * B :])
     s_lo, s_hi = blocks(s_lo[: 8 * B]), blocks(s_hi[: 8 * B])
@@ -360,8 +358,10 @@
     far, *rest = spread(hi, s_hi, t_hi, w)
     near, *parts = spread(lo, s_lo, t_lo, None)
     far = plus(far, *(blocks(r[: 2 * B]) for r in rest))
-    w = ring_sum(w, *(r[2 * B :] for r in rest), F32)
-    other = send(far, YN)
+    w = ring_sum(w, *(r[2 * B :] for r in rest))
+    other = send(carry(far, w), YN)
+    w = w.astype(F32) + other[2 * B :].astype(F32)
+    other = blocks(other[: 2 * B])
     got = send(w, CC)
     total = sum((t.astype(F32) for t in (near, *parts, other)), jnp.zeros((), F32))
     feature_grad = jnp.swapaxes(total, 1, 2).astype(BF16).reshape(2 * B, B)

time: 168 us -> 170 us (1.012)
  waiting for transfers between devices: 55.5 us -> 71.4 us
  starting transfers between devices: 51.3 us -> 41.9 us
  Pallas kernels: 51.4 us -> 45.9 us
    ppermute x34 -> x33, waiting for transfers between devices: 55.5 us -> 71.4 us  [send(): return lax.ppermute(value, AXES, pairs)]
    ppermute x34 -> x33, starting transfers between devices: 51.3 us -> 41.9 us  [send(): return lax.ppermute(value, AXES, pairs)]
    pallas_call x4, Pallas kernels: 28.1 us -> 23.8 us  [forward(): pl.pallas_call(functools.partial(_forward_kernel, chunk), name=f'tiles_fo...]
  transfers between devices with their start and end apart: 34 -> 33, of which waited for: 15 -> 21; matrix products, arithmetic and copies ran while one was open for 2% -> 2% of each run, Pallas kernels for 24% -> 19%
where the time goes in v1:
time: 170 us; the launch traced here: 167 us
  waiting for transfers between devices  71.4 us (42%)
  Pallas kernels  45.9 us (27%)
  starting transfers between devices  41.9 us (25%)
  other arithmetic  3.52 us (2%)
  local copies, waits for them, and re-layouts  2.41 us (1%)
    ppermute x33, waiting for transfers between devices, send(): return lax.ppermute(value, AXES, pairs)  71.4 us
    ppermute x33, starting transfers between devices, send(): return lax.ppermute(value, AXES, pairs)  41.9 us
    pallas_call x4, Pallas kernels, forward(): pl.pallas_call(functools.partial(_forward_kernel, chunk), name=f'tiles_fo...  23.8 us
    pallas_call x4, Pallas kernels, backward(): pl.pallas_call(functools.partial(_backward_kernel, chunk, len(adds)), nam...  20.7 us
  transfers between devices with their start and end apart: 33, of which 21 were waited for; matrix products, arithmetic and copies ran while one was open for 2% of the time, Pallas kernels for 19%

profile of v1, /device:TPU:0, one launch (start us, length us, event | category | flops | bytes accessed | tf_op | source)
XLA Modules:
  0.0 166.8 jit_solution(11142220060040070645)
XLA Ops:
  0.7 1.2 copy-done
  1.9 1.7 %collective-permute-start.5 = (bf16[2,256,256]{2,1,0:T(8,128)(2,1)S(1)}, bf16[2,256,256]{2,1,0:T(8,128)(2,1)S(1)}, u32[]{:S(2)}, u32[]{:S(2)}) collective-permute-start(bf16[2,256,256]{2,1,0:T(8,128)(2,1)S(1)} %constant_dynamic-slice_fusion), channel_id=1, source_target_pairs={{0,16},{1,17},{2,18},{3,19},{4,20},{5,21},{6,22},{7,23},{8,24},{9,... | collective-permute-start | bytes 786440 | tf_op jit(solution)/shard_map/ppermute | solution.py:51
  3.6 3.0 %collective-permute-start.2 = (bf16[2,256,256]{2,1,0:T(8,128)(2,1)S(1)}, bf16[2,256,256]{2,1,0:T(8,128)(2,1)S(1)}, u32[]{:S(2)}, u32[]{:S(2)}) collective-permute-start(bf16[2,256,256]{2,1,0:T(8,128)(2,1)S(1)} %constant_dynamic-slice_fusion), channel_id=1, source_target_pairs={{0,8},{1,65},{2,10},{3,67},{4,12},{5,69},{6,14},{7,71},{8,0},{9,73... | collective-permute-start | bytes 786440 | tf_op jit(solution)/shard_map/ppermute | solution.py:51
  6.6 1.1 collective-permute-start.1
  7.8 0.9 collective-permute-start
  8.7 1.3 collective-permute-done.5
  9.9 3.2 %collective-permute-start.8 = (bf16[2,256,256]{2,1,0:T(8,128)(2,1)S(1)}, bf16[2,256,256]{2,1,0:T(8,128)(2,1)S(1)}, u32[]{:S(2)}, u32[]{:S(2)}) collective-permute-start(bf16[2,256,256]{2,1,0:T(8,128)(2,1)S(1)} %collective-permute-done.5), channel_id=1, source_target_pairs={{0,8},{1,65},{2,10},{3,67},{4,12},{5,69},{6,14},{7,71},{8,0},{9,73... | collective-permute-start | bytes 786440 | tf_op jit(solution)/shard_map/ppermute | solution.py:51
  13.1 1.1 collective-permute-start.7
  14.3 0.9 collective-permute-start.6
  15.1 3.2 %collective-permute-start.9 = (bf16[2,256,256]{2,1,0:T(8,128)(2,1)}, bf16[2,256,256]{2,1,0:T(8,128)(2,1)S(1)}, u32[]{:S(2)}, u32[]{:S(2)}) collective-permute-start(bf16[2,256,256]{2,1,0:T(8,128)(2,1)} %bitcast.47), channel_id=1, source_target_pairs={{0,2},{1,3},{2,0},{3,1},{4,6},{5,7},{6,4},{7,5},{8,10},{9,11},{10,... | collective-permute-start | bytes 786440 | tf_op jit(solution)/shard_map/ppermute | solution.py:51
  18.5 4.1 %collective-permute-start.4 = (bf16[8,256,256]{2,1,0:T(8,128)(2,1)S(1)}, bf16[8,256,256]{2,1,0:T(8,128)(2,1)}, u32[]{:S(2)}, u32[]{:S(2)}) collective-permute-start(bf16[8,256,256]{2,1,0:T(8,128)(2,1)S(1)} %pad_maximum_fusion.fa), channel_id=1, source_target_pairs={{0,96},{1,13},{2,98},{3,15},{4,100},{5,1},{6,102},{7,3},{8,104},{9... | collective-permute-start | bytes 3145736 | tf_op jit(solution)/shard_map/ppermute | solution.py:51
  22.8 1.6 collective-permute-done.9.cot1
  24.3 3.2 %collective-permute-start.12 = (bf16[8,256,256]{2,1,0:T(8,128)(2,1)S(1)}, bf16[8,256,256]{2,1,0:T(8,128)(2,1)}, u32[]{:S(2)}, u32[]{:S(2)}) collective-permute-start(bf16[8,256,256]{2,1,0:T(8,128)(2,1)S(1)} %pad_maximum_fusion.1.fb), channel_id=1, source_target_pairs={{0,96},{1,13},{2,98},{3,15},{4,100},{5,1},{6,102},{7,3},{8,104},{9... | collective-permute-start | bytes 3145736 | tf_op jit(solution)/shard_map/ppermute | solution.py:51
  28.7 5.2 %tiles_forward_0.1.refs_0_ = f32[8,256,256]{2,1,0:T(8,128)S(1)} custom-call(s32[160]{0:T(256)S(1)} %select_reduce_fusion.1.tab, s32[9]{0:T(128)S(1)} %convert_reduce_fusion.3.offs, bf16[160,256,256]{2,1,0:T(8,128)(2,1)} %bitcast.49, bf16[8,256,256]{2,1,0:T(8,128)(2,1)S(1)} %pad_maximum_fusion.fa, bf16[8,256,256]{2,1,0:T(8,128)(2,1)S(1)} %pad_maximum_fusion.1.fb), custom_call_target="tpu_custom_call" | custom-call | flops 16777216 | bytes 65536 | tf_op jit(solution)/shard_map/tiles_forward_0/pallas_call | solution.py:174
  33.9 1.0 collective-permute-done.4.fb
  34.9 3.8 %collective-permute-done.3.fa = bf16[8,256,256]{2,1,0:T(8,128)(2,1)} collective-permute-done((bf16[8,256,256]{2,1,0:T(8,128)(2,1)S(1)}, bf16[8,256,256]{2,1,0:T(8,128)(2,1)}, u32[]{:S(2)}, u32[]{:S(2)}) %collective-permute-start.3) | collective-permute-done | bytes 1048608 | tf_op jit(solution)/shard_map/ppermute | solution.py:51
  38.7 5.4 %tiles_forward_1.1.refs_0_ = f32[8,256,256]{2,1,0:T(8,128)S(1)} custom-call(s32[160]{0:T(256)S(1)} %select_reduce_fusion.1.tab, s32[9]{0:T(128)S(1)} %convert_reduce_fusion.3.offs, bf16[160,256,256]{2,1,0:T(8,128)(2,1)} %bitcast.50, bf16[8,256,256]{2,1,0:T(8,128)(2,1)} %collective-permute-done.3.fa, ...), custom_call_target="tpu_custom_call", output_to_operand_aliasing={{}: (5, {})} | custom-call | flops 16777216 | bytes 65536 | tf_op jit(solution)/shard_map/tiles_forward_1/pallas_call | solution.py:174
  44.1 2.0 %collective-permute-done.12.fb = bf16[8,256,256]{2,1,0:T(8,128)(2,1)} collective-permute-done((bf16[8,256,256]{2,1,0:T(8,128)(2,1)S(1)}, bf16[8,256,256]{2,1,0:T(8,128)(2,1)}, u32[]{:S(2)}, u32[]{:S(2)}) %collective-permute-start.12) | collective-permute-done | bytes 1048608 | tf_op jit(solution)/shard_map/ppermute | solution.py:51
  46.2 3.8 %collective-permute-done.11.fa = bf16[8,256,256]{2,1,0:T(8,128)(2,1)} collective-permute-done((bf16[8,256,256]{2,1,0:T(8,128)(2,1)S(1)}, bf16[8,256,256]{2,1,0:T(8,128)(2,1)}, u32[]{:S(2)}, u32[]{:S(2)}) %collective-permute-start.11) | collective-permute-done | bytes 1048608 | tf_op jit(solution)/shard_map/ppermute | solution.py:51
  50.0 7.0 %tiles_forward_2.1.refs_0_ = f32[8,256,256]{2,1,0:T(8,128)S(1)} custom-call(s32[160]{0:T(256)S(1)} %select_reduce_fusion.1.tab, s32[9]{0:T(128)S(1)} %convert_reduce_fusion.3.offs, bf16[160,256,256]{2,1,0:T(8,128)(2,1)} %bitcast.51, bf16[8,256,256]{2,1,0:T(8,128)(2,1)} %collective-permute-done.11.fa, ...), custom_call_target="tpu_custom_call", output_to_operand_aliasing={{}: (5, {})} | custom-call | flops 16777216 | bytes 65536 | tf_op jit(solution)/shard_map/tiles_forward_2/pallas_call | solution.py:174
  56.9 4.2 %collective-permute-done.10.fa = bf16[8,256,256]{2,1,0:T(8,128)(2,1)S(1)} collective-permute-done((bf16[8,256,256]{2,1,0:T(8,128)(2,1)}, bf16[8,256,256]{2,1,0:T(8,128)(2,1)S(1)}, u32[]{:S(2)}, u32[]{:S(2)}) %collective-permute-start.10) | collective-permute-done | bytes 1048608 | tf_op jit(solution)/shard_map/ppermute | solution.py:51
  61.1 3.9 %collective-permute-done.13.fb = bf16[8,256,256]{2,1,0:T(8,128)(2,1)S(1)} collective-permute-done((bf16[8,256,256]{2,1,0:T(8,128)(2,1)}, bf16[8,256,256]{2,1,0:T(8,128)(2,1)S(1)}, u32[]{:S(2)}, u32[]{:S(2)}) %collective-permute-start.13) | collective-permute-done | bytes 1048608 | tf_op jit(solution)/shard_map/ppermute | solution.py:51
  65.0 6.2 %tiles_forward_3.1 = f32[8,256,256]{2,1,0:T(8,128)S(1)} custom-call(s32[160]{0:T(256)S(1)} %select_reduce_fusion.1.tab, s32[9]{0:T(128)S(1)} %convert_reduce_fusion.3.offs, bf16[160,256,256]{2,1,0:T(8,128)(2,1)} %bitcast.52, bf16[8,256,256]{2,1,0:T(8,128)(2,1)S(1)} %collective-permute-done.10.fa, ...), custom_call_target="tpu_custom_call", output_to_operand_aliasing={{}: (5, {})} | custom-call | flops 16777216 | bytes 65536 | tf_op jit(solution)/shard_map/tiles_forward_3/pallas_call | solution.py:174
  71.4 2.6 %collective-permute-done.14 = f32[4,256,256]{2,1,0:T(8,128)S(1)} collective-permute-done((f32[4,256,256]{2,1,0:T(8,128)S(1)}, f32[4,256,256]{2,1,0:T(8,128)S(1)}, u32[]{:S(2)}, u32[]{:S(2)}) %collective-permute-start.14) | collective-permute-done | bytes 1048608 | tf_op jit(solution)/shard_map/ppermute | solution.py:51
  75.2 14.7 %collective-permute-done.15.far = bf16[4,256,256]{2,1,0:T(8,128)(2,1)S(1)} collective-permute-done((bf16[4,256,256]{2,1,0:T(8,128)(2,1)S(1)}, bf16[4,256,256]{2,1,0:T(8,128)(2,1)S(1)}, u32[]{:S(2)}, u32[]{:S(2)}) %collective-permute-start.15) | collective-permute-done | bytes 524320 | tf_op jit(solution)/shard_map/ppermute | solution.py:51
  89.9 1.4 dense.1
  92.2 1.2 collective-permute-done.17
  93.4 6.3 %tiles_backward_3.1 = (bf16[8,256,256]{2,1,0:T(8,128)(2,1)}, bf16[8,256,256]{2,1,0:T(8,128)(2,1)}) custom-call(s32[160]{0:T(256)S(1)} %select_reduce_fusion.tab, s32[9]{0:T(128)S(1)} %convert_reduce_fusion.2.offs, bf16[160,256,256]{2,1,0:T(8,128)(2,1)} %bitcast.53, bf16[4,256,256]{2,1,0:T(8,128)(2,1)S(1)} %get-tuple-element.64.d0, ...), custom_call_target="tpu_custom_call" | custom-call | flops 16777216 | bytes 65536 | tf_op jit(solution)/shard_map/tiles_backward_3/pallas_call | solution.py:223
  99.8 3.2 %collective-permute-start.19 = (bf16[8,256,256]{2,1,0:T(8,128)(2,1)}, bf16[8,256,256]{2,1,0:T(8,128)(2,1)}, u32[]{:S(2)}, u32[]{:S(2)}) collective-permute-start(bf16[8,256,256]{2,1,0:T(8,128)(2,1)} %get-tuple-element.51), channel_id=1, source_target_pairs={{0,96},{1,13},{2,98},{3,15},{4,100},{5,1},{6,102},{7,3},{8,104},{9... | collective-permute-start | bytes 3145736 | tf_op jit(solution)/shard_map/ppermute | solution.py:51
  103.0 4.7 %tiles_backward_1.1 = (bf16[2176,256]{1,0:T(8,128)(2,1)S(1)}, bf16[2176,256]{1,0:T(8,128)(2,1)S(1)}) custom-call(s32[160]{0:T(256)S(1)} %select_reduce_fusion.tab, s32[9]{0:T(128)S(1)} %convert_reduce_fusion.2.offs, bf16[160,256,256]{2,1,0:T(8,128)(2,1)} %bitcast.54, bf16[4,256,256]{2,1,0:T(8,128)(2,1)S(1)} %get-tuple-element.64.d0, ...), custom_call_target="tpu_custom_call" | custom-call | flops 16777216 | bytes 65536 | tf_op jit(solution)/shard_map/tiles_backward_1/pallas_call | solution.py:223
  108.3 1.5 collective-permute-start.21
  109.8 6.1 %collective-permute-done.18.refs_1_ = bf16[8,256,256]{2,1,0:T(8,128)(2,1)S(1)} collective-permute-done((bf16[8,256,256]{2,1,0:T(8,128)(2,1)}, bf16[8,256,256]{2,1,0:T(8,128)(2,1)S(1)}, u32[]{:S(2)}, u32[]{:S(2)}) %collective-permute-start.18) | collective-permute-done | bytes 1048608 | tf_op jit(solution)/shard_map/ppermute | solution.py:51
  116.0 5.1 %tiles_backward_2.1 = (bf16[8,256,256]{2,1,0:T(8,128)(2,1)S(1)}, bf16[8,256,256]{2,1,0:T(8,128)(2,1)S(1)}) custom-call(s32[160]{0:T(256)S(1)} %select_reduce_fusion.tab, s32[9]{0:T(128)S(1)} %convert_reduce_fusion.2.offs, bf16[160,256,256]{2,1,0:T(8,128)(2,1)} %bitcast.55, bf16[4,256,256]{2,1,0:T(8,128)(2,1)S(1)} %get-tuple-element.64.d0, ...), custom_call_target="tpu_custom_call" | custom-call | flops 16777216 | bytes 65536 | tf_op jit(solution)/shard_map/tiles_backward_2/pallas_call | solution.py:223
  121.1 3.0 %collective-permute-start.27 = (bf16[8,256,256]{2,1,0:T(8,128)(2,1)S(1)}, bf16[8,256,256]{2,1,0:T(8,128)(2,1)S(1)}, u32[]{:S(2)}, u32[]{:S(2)}) collective-permute-start(bf16[8,256,256]{2,1,0:T(8,128)(2,1)S(1)} %get-tuple-element.62), channel_id=1, source_target_pairs={{0,96},{1,13},{2,98},{3,15},{4,100},{5,1},{6,102},{7,3},{8,104},{9... | collective-permute-start | bytes 3145736 | tf_op jit(solution)/shard_map/ppermute | solution.py:51
  124.1 0.9 collective-permute-start.23
  125.1 4.6 %tiles_backward_0.1 = (bf16[8,256,256]{2,1,0:T(8,128)(2,1)S(1)}, bf16[8,256,256]{2,1,0:T(8,128)(2,1)S(1)}) custom-call(s32[160]{0:T(256)S(1)} %select_reduce_fusion.tab, s32[9]{0:T(128)S(1)} %convert_reduce_fusion.2.offs, bf16[160,256,256]{2,1,0:T(8,128)(2,1)} %bitcast.56, bf16[4,256,256]{2,1,0:T(8,128)(2,1)S(1)} %get-tuple-element.64.d0, ...), custom_call_target="tpu_custom_call" | custom-call | flops 16777216 | bytes 65536 | tf_op jit(solution)/shard_map/tiles_backward_0/pallas_call | solution.py:223
  130.2 9.2 %collective-permute-done.27 = bf16[8,256,256]{2,1,0:T(8,128)(2,1)S(1)} collective-permute-done((bf16[8,256,256]{2,1,0:T(8,128)(2,1)S(1)}, bf16[8,256,256]{2,1,0:T(8,128)(2,1)S(1)}, u32[]{:S(2)}, u32[]{:S(2)}) %collective-permute-start.27) | collective-permute-done | bytes 1048608 | tf_op jit(solution)/shard_map/ppermute | solution.py:51
  139.8 0.8 collective-permute-start.28
  140.6 2.9 %collective-permute-start.29 = (bf16[640,256]{1,0:T(8,128)(2,1)S(1)}, bf16[640,256]{1,0:T(8,128)(2,1)S(1)}, u32[]{:S(2)}, u32[]{:S(2)}) collective-permute-start(bf16[640,256]{1,0:T(8,128)(2,1)S(1)} %get-tuple-element.96), channel_id=1, source_target_pairs={{0,4},{1,33},{2,6},{3,35},{4,8},{5,37},{6,10},{7,39},{8,12},{9,41}... | collective-permute-start | bytes 983048 | tf_op jit(solution)/shard_map/ppermute | solution.py:51
  144.1 4.4 %collective-permute-done.28 = bf16[640,256]{1,0:T(8,128)(2,1)S(1)} collective-permute-done((bf16[640,256]{1,0:T(8,128)(2,1)S(1)}, bf16[640,256]{1,0:T(8,128)(2,1)S(1)}, u32[]{:S(2)}, u32[]{:S(2)}) %collective-permute-start.28) | collective-permute-done | bytes 327712 | tf_op jit(solution)/shard_map/ppermute | solution.py:51
  148.6 3.4 %collective-permute-done.29 = bf16[640,256]{1,0:T(8,128)(2,1)S(1)} collective-permute-done((bf16[640,256]{1,0:T(8,128)(2,1)S(1)}, bf16[640,256]{1,0:T(8,128)(2,1)S(1)}, u32[]{:S(2)}, u32[]{:S(2)}) %collective-permute-start.29) | collective-permute-done | bytes 327712 | tf_op jit(solution)/shard_map/ppermute | solution.py:51
  152.4 1.5 collective-permute-start.31
  155.0 2.0 %collective-permute-start.26 = (bf16[2,256,256]{2,1,0:T(8,128)(2,1)S(1)}, bf16[2,256,256]{2,1,0:T(8,128)(2,1)S(1)}, u32[]{:S(2)}, u32[]{:S(2)}) collective-permute-start(bf16[2,256,256]{2,1,0:T(8,128)(2,1)S(1)} %get-tuple-element.82), channel_id=1, source_target_pairs={{0,12},{1,97},{2,14},{3,99},{4,0},{5,101},{6,2},{7,103},{8,4},{9,1... | collective-permute-start | bytes 786440 | tf_op jit(solution)/shard_map/ppermute | solution.py:51
  157.1 3.4 %collective-permute-done.31 = bf16[640,256]{1,0:T(8,128)(2,1)S(1)} collective-permute-done((bf16[640,256]{1,0:T(8,128)(2,1)S(1)}, bf16[640,256]{1,0:T(8,128)(2,1)S(1)}, u32[]{:S(2)}, u32[]{:S(2)}) %collective-permute-start.31) | collective-permute-done | bytes 327712 | tf_op jit(solution)/shard_map/ppermute | solution.py:51
  160.6 1.6 collective-permute-done.24
  162.2 1.4 collective-permute-done.26
  163.6 1.4 collective-permute-done.25
  165.2 0.8 copy.14
  (70 shorter events, 7.9 us)
Async XLA Ops:
  0.6 1.2 copy-start
  1.9 8.0 %collective-permute-start.5 = (bf16[2,256,256]{2,1,0:T(8,128)(2,1)S(1)}, bf16[2,256,256]{2,1,0:T(8,128)(2,1)S(1)}, u32[]{:S(2)}, u32[]{:S(2)}) collective-permute-start(bf16[2,256,256]{2,1,0:T(8,128)(2,1)S(1)} %constant_dynamic-slice_fusion), channel_id=1, source_target_pairs={{0,16},{1,17},{2,18},{3,19},{4,20},{5,21},{6,22},{7,23},{8,24},{9,... | collective-permute-start | bytes 786440 | tf_op jit(solution)/shard_map/ppermute | solution.py:51
  3.6 10.6 %collective-permute-start.2 = (bf16[2,256,256]{2,1,0:T(8,128)(2,1)S(1)}, bf16[2,256,256]{2,1,0:T(8,128)(2,1)S(1)}, u32[]{:S(2)}, u32[]{:S(2)}) collective-permute-start(bf16[2,256,256]{2,1,0:T(8,128)(2,1)S(1)} %constant_dynamic-slice_fusion), channel_id=1, source_target_pairs={{0,8},{1,65},{2,10},{3,67},{4,12},{5,69},{6,14},{7,71},{8,0},{9,73... | collective-permute-start | bytes 786440 | tf_op jit(solution)/shard_map/ppermute | solution.py:51
  6.6 8.5 %collective-permute-start.1 = (bf16[2,256,256]{2,1,0:T(8,128)(2,1)S(1)}, bf16[2,256,256]{2,1,0:T(8,128)(2,1)S(1)}, u32[]{:S(2)}, u32[]{:S(2)}) collective-permute-start(bf16[2,256,256]{2,1,0:T(8,128)(2,1)S(1)} %constant_dynamic-slice_fusion), channel_id=1, source_target_pairs={{0,12},{1,97},{2,14},{3,99},{4,0},{5,101},{6,2},{7,103},{8,4},{9,1... | collective-permute-start | bytes 786440 | tf_op jit(solution)/shard_map/ppermute | solution.py:51
  7.8 10.6 %collective-permute-start = (bf16[2,256,256]{2,1,0:T(8,128)(2,1)S(1)}, bf16[2,256,256]{2,1,0:T(8,128)(2,1)S(1)}, u32[]{:S(2)}, u32[]{:S(2)}) collective-permute-start(bf16[2,256,256]{2,1,0:T(8,128)(2,1)S(1)} %constant_dynamic-slice_fusion), channel_id=1, source_target_pairs={{0,4},{1,33},{2,6},{3,35},{4,8},{5,37},{6,10},{7,39},{8,12},{9,41}... | collective-permute-start | bytes 786440 | tf_op jit(solution)/shard_map/ppermute | solution.py:51
  9.9 12.7 %collective-permute-start.8 = (bf16[2,256,256]{2,1,0:T(8,128)(2,1)S(1)}, bf16[2,256,256]{2,1,0:T(8,128)(2,1)S(1)}, u32[]{:S(2)}, u32[]{:S(2)}) collective-permute-start(bf16[2,256,256]{2,1,0:T(8,128)(2,1)S(1)} %collective-permute-done.5), channel_id=1, source_target_pairs={{0,8},{1,65},{2,10},{3,67},{4,12},{5,69},{6,14},{7,71},{8,0},{9,73... | collective-permute-start | bytes 786440 | tf_op jit(solution)/shard_map/ppermute | solution.py:51
  13.1 9.5 %collective-permute-start.7 = (bf16[2,256,256]{2,1,0:T(8,128)(2,1)S(1)}, bf16[2,256,256]{2,1,0:T(8,128)(2,1)S(1)}, u32[]{:S(2)}, u32[]{:S(2)}) collective-permute-start(bf16[2,256,256]{2,1,0:T(8,128)(2,1)S(1)} %collective-permute-done.5), channel_id=1, source_target_pairs={{0,12},{1,97},{2,14},{3,99},{4,0},{5,101},{6,2},{7,103},{8,4},{9,1... | collective-permute-start | bytes 786440 | tf_op jit(solution)/shard_map/ppermute | solution.py:51
  14.3 8.4 %collective-permute-start.6 = (bf16[2,256,256]{2,1,0:T(8,128)(2,1)S(1)}, bf16[2,256,256]{2,1,0:T(8,128)(2,1)S(1)}, u32[]{:S(2)}, u32[]{:S(2)}) collective-permute-start(bf16[2,256,256]{2,1,0:T(8,128)(2,1)S(1)} %collective-permute-done.5), channel_id=1, source_target_pairs={{0,4},{1,33},{2,6},{3,35},{4,8},{5,37},{6,10},{7,39},{8,12},{9,41}... | collective-permute-start | bytes 786440 | tf_op jit(solution)/shard_map/ppermute | solution.py:51
  15.1 9.2 %collective-permute-start.9 = (bf16[2,256,256]{2,1,0:T(8,128)(2,1)}, bf16[2,256,256]{2,1,0:T(8,128)(2,1)S(1)}, u32[]{:S(2)}, u32[]{:S(2)}) collective-permute-start(bf16[2,256,256]{2,1,0:T(8,128)(2,1)} %bitcast.47), channel_id=1, source_target_pairs={{0,2},{1,3},{2,0},{3,1},{4,6},{5,7},{6,4},{7,5},{8,10},{9,11},{10,... | collective-permute-start | bytes 786440 | tf_op jit(solution)/shard_map/ppermute | solution.py:51
  18.5 9.7 %copy-start.3 = (s32[1,1,160]{2,1,0:T(1,128)S(1)}, s32[1,1,160]{2,1,0:T(1,128)}, u32[]{:S(2)}) copy-start(s32[1,1,160]{2,1,0:T(1,128)} %param.12) | copy-start | bytes 1924
  18.5 9.7 %copy-start.4 = (s32[1,1,160]{2,1,0:T(1,128)S(1)}, s32[1,1,160]{2,1,0:T(1,128)}, u32[]{:S(2)}) copy-start(s32[1,1,160]{2,1,0:T(1,128)} %param.11) | copy-start | bytes 1924
  18.5 16.4 %collective-permute-start.4 = (bf16[8,256,256]{2,1,0:T(8,128)(2,1)S(1)}, bf16[8,256,256]{2,1,0:T(8,128)(2,1)}, u32[]{:S(2)}, u32[]{:S(2)}) collective-permute-start(bf16[8,256,256]{2,1,0:T(8,128)(2,1)S(1)} %pad_maximum_fusion.fa), channel_id=1, source_target_pairs={{0,96},{1,13},{2,98},{3,15},{4,100},{5,1},{6,102},{7,3},{8,104},{9... | collective-permute-start | bytes 3145736 | tf_op jit(solution)/shard_map/ppermute | solution.py:51
  22.6 16.1 %collective-permute-start.3 = (bf16[8,256,256]{2,1,0:T(8,128)(2,1)S(1)}, bf16[8,256,256]{2,1,0:T(8,128)(2,1)}, u32[]{:S(2)}, u32[]{:S(2)}) collective-permute-start(bf16[8,256,256]{2,1,0:T(8,128)(2,1)S(1)} %pad_maximum_fusion.fa), channel_id=1, source_target_pairs={{0,32},{1,5},{2,34},{3,7},{4,36},{5,9},{6,38},{7,11},{8,40},{9,13}... | collective-permute-start | bytes 3145736 | tf_op jit(solution)/shard_map/ppermute | solution.py:51
  24.3 21.8 %collective-permute-start.12 = (bf16[8,256,256]{2,1,0:T(8,128)(2,1)S(1)}, bf16[8,256,256]{2,1,0:T(8,128)(2,1)}, u32[]{:S(2)}, u32[]{:S(2)}) collective-permute-start(bf16[8,256,256]{2,1,0:T(8,128)(2,1)S(1)} %pad_maximum_fusion.1.fb), channel_id=1, source_target_pairs={{0,96},{1,13},{2,98},{3,15},{4,100},{5,1},{6,102},{7,3},{8,104},{9... | collective-permute-start | bytes 3145736 | tf_op jit(solution)/shard_map/ppermute | solution.py:51
  27.5 22.4 %collective-permute-start.11 = (bf16[8,256,256]{2,1,0:T(8,128)(2,1)S(1)}, bf16[8,256,256]{2,1,0:T(8,128)(2,1)}, u32[]{:S(2)}, u32[]{:S(2)}) collective-permute-start(bf16[8,256,256]{2,1,0:T(8,128)(2,1)S(1)} %pad_maximum_fusion.1.fb), channel_id=1, source_target_pairs={{0,32},{1,5},{2,34},{3,7},{4,36},{5,9},{6,38},{7,11},{8,40},{9,13}... | collective-permute-start | bytes 3145736 | tf_op jit(solution)/shard_map/ppermute | solution.py:51
  38.7 22.4 %collective-permute-start.10 = (bf16[8,256,256]{2,1,0:T(8,128)(2,1)}, bf16[8,256,256]{2,1,0:T(8,128)(2,1)S(1)}, u32[]{:S(2)}, u32[]{:S(2)}) collective-permute-start(bf16[8,256,256]{2,1,0:T(8,128)(2,1)} %collective-permute-done.3.fa), channel_id=1, source_target_pairs={{0,32},{1,5},{2,34},{3,7},{4,36},{5,9},{6,38},{7,11},{8,40},{9,13}... | collective-permute-start | bytes 3145736 | tf_op jit(solution)/shard_map/ppermute | solution.py:51
  50.0 15.0 %collective-permute-start.13 = (bf16[8,256,256]{2,1,0:T(8,128)(2,1)}, bf16[8,256,256]{2,1,0:T(8,128)(2,1)S(1)}, u32[]{:S(2)}, u32[]{:S(2)}) collective-permute-start(bf16[8,256,256]{2,1,0:T(8,128)(2,1)} %collective-permute-done.12.fb), channel_id=1, source_target_pairs={{0,96},{1,13},{2,98},{3,15},{4,100},{5,1},{6,102},{7,3},{8,104},{9... | collective-permute-start | bytes 3145736 | tf_op jit(solution)/shard_map/ppermute | solution.py:51
  71.3 18.6 %copy-start.1 = (bf16[512,256]{1,0:T(8,128)(2,1)S(1)}, bf16[512,256]{1,0:T(8,128)(2,1)}, u32[]{:S(2)}) copy-start(bf16[512,256]{1,0:T(8,128)(2,1)} %param.9) | copy-start | bytes 786436
  71.3 18.5 %copy-start.2 = (bf16[256,256]{1,0:T(8,128)(2,1)S(1)}, bf16[256,256]{1,0:T(8,128)(2,1)}, u32[]{:S(2)}) copy-start(bf16[256,256]{1,0:T(8,128)(2,1)} %w_ref.1) | copy-start | bytes 393220
  71.3 2.7 %collective-permute-start.14 = (f32[4,256,256]{2,1,0:T(8,128)S(1)}, f32[4,256,256]{2,1,0:T(8,128)S(1)}, u32[]{:S(2)}, u32[]{:S(2)}) collective-permute-start(f32[4,256,256]{2,1,0:T(8,128)S(1)} %slice.171), channel_id=1, source_target_pairs={{0,1},{1,0},{2,3},{3,2},{4,5},{5,4},{6,7},{7,6},{8,9},{9,8},{10,11... | collective-permute-start | bytes 3145736 | tf_op jit(solution)/shard_map/ppermute | solution.py:51
  74.3 15.5 %collective-permute-start.15 = (bf16[4,256,256]{2,1,0:T(8,128)(2,1)S(1)}, bf16[4,256,256]{2,1,0:T(8,128)(2,1)S(1)}, u32[]{:S(2)}, u32[]{:S(2)}) collective-permute-start(bf16[4,256,256]{2,1,0:T(8,128)(2,1)S(1)} %fusion.near), channel_id=1, source_target_pairs={{0,2},{1,3},{2,0},{3,1},{4,6},{5,7},{6,4},{7,5},{8,10},{9,11},{10,... | collective-permute-start | bytes 1572872 | tf_op jit(solution)/shard_map/ppermute | solution.py:51
  91.3 2.1 %collective-permute-start.16 = (bf16[4,256,256]{2,1,0:T(8,128)(2,1)S(1)}, bf16[4,256,256]{2,1,0:T(8,128)(2,1)S(1)}, u32[]{:S(2)}, u32[]{:S(2)}) collective-permute-start(bf16[4,256,256]{2,1,0:T(8,128)(2,1)S(1)} %get-tuple-element.64.d0), channel_id=1, source_target_pairs={{0,1},{1,0},{2,3},{3,2},{4,5},{5,4},{6,7},{7,6},{8,9},{9,8},{10,11... | collective-permute-start | bytes 1572872 | tf_op jit(solution)/shard_map/ppermute | solution.py:51
  91.3 2.0 %collective-permute-start.17 = (f32[128,256]{1,0:T(8,128)S(1)}, f32[128,256]{1,0:T(8,128)S(1)}, u32[]{:S(2)}, u32[]{:S(2)}) collective-permute-start(f32[128,256]{1,0:T(8,128)S(1)} %dynamic-slice_bitcast_fusion), channel_id=1, source_target_pairs={{0,1},{1,0},{2,3},{3,2},{4,5},{5,4},{6,7},{7,6},{8,9},{9,8},{10,11... | collective-permute-start | bytes 393224 | tf_op jit(solution)/shard_map/ppermute | solution.py:51
  99.7 16.3 %collective-permute-start.18 = (bf16[8,256,256]{2,1,0:T(8,128)(2,1)}, bf16[8,256,256]{2,1,0:T(8,128)(2,1)S(1)}, u32[]{:S(2)}, u32[]{:S(2)}) collective-permute-start(bf16[8,256,256]{2,1,0:T(8,128)(2,1)} %get-tuple-element.50), channel_id=1, source_target_pairs={{0,32},{1,5},{2,34},{3,7},{4,36},{5,9},{6,38},{7,11},{8,40},{9,13}... | collective-permute-start | bytes 3145736 | tf_op jit(solution)/shard_map/ppermute | solution.py:51
  99.8 16.2 %collective-permute-start.19 = (bf16[8,256,256]{2,1,0:T(8,128)(2,1)}, bf16[8,256,256]{2,1,0:T(8,128)(2,1)}, u32[]{:S(2)}, u32[]{:S(2)}) collective-permute-start(bf16[8,256,256]{2,1,0:T(8,128)(2,1)} %get-tuple-element.51), channel_id=1, source_target_pairs={{0,96},{1,13},{2,98},{3,15},{4,100},{5,1},{6,102},{7,3},{8,104},{9... | collective-permute-start | bytes 3145736 | tf_op jit(solution)/shard_map/ppermute | solution.py:51
  107.7 22.2 %collective-permute-start.20 = (bf16[2176,256]{1,0:T(8,128)(2,1)S(1)}, bf16[2176,256]{1,0:T(8,128)(2,1)S(1)}, u32[]{:S(2)}, u32[]{:S(2)}) collective-permute-start(bf16[2176,256]{1,0:T(8,128)(2,1)S(1)} %get-tuple-element.56), channel_id=1, source_target_pairs={{0,96},{1,13},{2,98},{3,15},{4,100},{5,1},{6,102},{7,3},{8,104},{9... | collective-permute-start | bytes 3342344 | tf_op jit(solution)/shard_map/ppermute | solution.py:51
  108.3 21.7 %collective-permute-start.21 = (bf16[2176,256]{1,0:T(8,128)(2,1)S(1)}, bf16[2176,256]{1,0:T(8,128)(2,1)S(1)}, u32[]{:S(2)}, u32[]{:S(2)}) collective-permute-start(bf16[2176,256]{1,0:T(8,128)(2,1)S(1)} %get-tuple-element.57), channel_id=1, source_target_pairs={{0,32},{1,5},{2,34},{3,7},{4,36},{5,9},{6,38},{7,11},{8,40},{9,13}... | collective-permute-start | bytes 3342344 | tf_op jit(solution)/shard_map/ppermute | solution.py:51
  121.1 18.3 %collective-permute-start.27 = (bf16[8,256,256]{2,1,0:T(8,128)(2,1)S(1)}, bf16[8,256,256]{2,1,0:T(8,128)(2,1)S(1)}, u32[]{:S(2)}, u32[]{:S(2)}) collective-permute-start(bf16[8,256,256]{2,1,0:T(8,128)(2,1)S(1)} %get-tuple-element.62), channel_id=1, source_target_pairs={{0,96},{1,13},{2,98},{3,15},{4,100},{5,1},{6,102},{7,3},{8,104},{9... | collective-permute-start | bytes 3145736 | tf_op jit(solution)/shard_map/ppermute | solution.py:51
  124.1 5.9 %collective-permute-start.22 = (bf16[128,256]{1,0:T(8,128)(2,1)S(1)}, bf16[128,256]{1,0:T(8,128)(2,1)S(1)}, u32[]{:S(2)}, u32[]{:S(2)}) collective-permute-start(bf16[128,256]{1,0:T(8,128)(2,1)S(1)} %fusion.21.refs_0_), channel_id=1, source_target_pairs={{0,64},{1,9},{2,66},{3,11},{4,68},{5,13},{6,70},{7,15},{8,72},{9,1... | collective-permute-start | bytes 196616 | tf_op jit(solution)/shard_map/ppermute | solution.py:51
  124.1 29.8 %collective-permute-start.23 = (bf16[8,256,256]{2,1,0:T(8,128)(2,1)S(1)}, bf16[8,256,256]{2,1,0:T(8,128)(2,1)S(1)}, u32[]{:S(2)}, u32[]{:S(2)}) collective-permute-start(bf16[8,256,256]{2,1,0:T(8,128)(2,1)S(1)} %get-tuple-element.63), channel_id=1, source_target_pairs={{0,32},{1,5},{2,34},{3,7},{4,36},{5,9},{6,38},{7,11},{8,40},{9,13}... | collective-permute-start | bytes 3145736 | tf_op jit(solution)/shard_map/ppermute | solution.py:51
  139.8 8.8 %collective-permute-start.28 = (bf16[640,256]{1,0:T(8,128)(2,1)S(1)}, bf16[640,256]{1,0:T(8,128)(2,1)S(1)}, u32[]{:S(2)}, u32[]{:S(2)}) collective-permute-start(bf16[640,256]{1,0:T(8,128)(2,1)S(1)} %get-tuple-element.95), channel_id=1, source_target_pairs={{0,8},{1,65},{2,10},{3,67},{4,12},{5,69},{6,14},{7,71},{8,0},{9,73... | collective-permute-start | bytes 983048 | tf_op jit(solution)/shard_map/ppermute | solution.py:51
  140.6 11.3 %collective-permute-start.29 = (bf16[640,256]{1,0:T(8,128)(2,1)S(1)}, bf16[640,256]{1,0:T(8,128)(2,1)S(1)}, u32[]{:S(2)}, u32[]{:S(2)}) collective-permute-start(bf16[640,256]{1,0:T(8,128)(2,1)S(1)} %get-tuple-element.96), channel_id=1, source_target_pairs={{0,4},{1,33},{2,6},{3,35},{4,8},{5,37},{6,10},{7,39},{8,12},{9,41}... | collective-permute-start | bytes 983048 | tf_op jit(solution)/shard_map/ppermute | solution.py:51
  143.5 8.6 %collective-permute-start.30 = (bf16[640,256]{1,0:T(8,128)(2,1)S(1)}, bf16[640,256]{1,0:T(8,128)(2,1)S(1)}, u32[]{:S(2)}, u32[]{:S(2)}) collective-permute-start(bf16[640,256]{1,0:T(8,128)(2,1)S(1)} %get-tuple-element.97), channel_id=1, source_target_pairs={{0,12},{1,97},{2,14},{3,99},{4,0},{5,101},{6,2},{7,103},{8,4},{9,1... | collective-permute-start | bytes 983048 | tf_op jit(solution)/shard_map/ppermute | solution.py:51
  152.4 8.1 %collective-permute-start.31 = (bf16[640,256]{1,0:T(8,128)(2,1)S(1)}, bf16[640,256]{1,0:T(8,128)(2,1)S(1)}, u32[]{:S(2)}, u32[]{:S(2)}) collective-permute-start(bf16[640,256]{1,0:T(8,128)(2,1)S(1)} %pad_maximum_fusion.5), channel_id=1, source_target_pairs={{0,16},{1,17},{2,18},{3,19},{4,20},{5,21},{6,22},{7,23},{8,24},{9,... | collective-permute-start | bytes 983048 | tf_op jit(solution)/shard_map/ppermute | solution.py:51
  154.2 8.0 %collective-permute-start.24 = (bf16[2,256,256]{2,1,0:T(8,128)(2,1)S(1)}, bf16[2,256,256]{2,1,0:T(8,128)(2,1)S(1)}, u32[]{:S(2)}, u32[]{:S(2)}) collective-permute-start(bf16[2,256,256]{2,1,0:T(8,128)(2,1)S(1)} %get-tuple-element.81), channel_id=1, source_target_pairs={{0,8},{1,65},{2,10},{3,67},{4,12},{5,69},{6,14},{7,71},{8,0},{9,73... | collective-permute-start | bytes 786440 | tf_op jit(solution)/shard_map/ppermute | solution.py:51
  155.0 8.6 %collective-permute-start.26 = (bf16[2,256,256]{2,1,0:T(8,128)(2,1)S(1)}, bf16[2,256,256]{2,1,0:T(8,128)(2,1)S(1)}, u32[]{:S(2)}, u32[]{:S(2)}) collective-permute-start(bf16[2,256,256]{2,1,0:T(8,128)(2,1)S(1)} %get-tuple-element.82), channel_id=1, source_target_pairs={{0,12},{1,97},{2,14},{3,99},{4,0},{5,101},{6,2},{7,103},{8,4},{9,1... | collective-permute-start | bytes 786440 | tf_op jit(solution)/shard_map/ppermute | solution.py:51
  157.1 8.0 %collective-permute-start.25 = (bf16[2,256,256]{2,1,0:T(8,128)(2,1)S(1)}, bf16[2,256,256]{2,1,0:T(8,128)(2,1)S(1)}, u32[]{:S(2)}, u32[]{:S(2)}) collective-permute-start(bf16[2,256,256]{2,1,0:T(8,128)(2,1)S(1)} %get-tuple-element.83), channel_id=1, source_target_pairs={{0,4},{1,33},{2,6},{3,35},{4,8},{5,37},{6,10},{7,39},{8,12},{9,41}... | collective-permute-start | bytes 786440 | tf_op jit(solution)/shard_map/ppermute | solution.py:51
  160.5 5.6 %collective-permute-start.32 = (f32[128,256]{1,0:T(8,128)S(1)}, f32[128,256]{1,0:T(8,128)S(1)}, u32[]{:S(2)}, u32[]{:S(2)}) collective-permute-start(f32[128,256]{1,0:T(8,128)S(1)} %convert_add_fusion.12), channel_id=1, source_target_pairs={{0,1},{1,0},{2,3},{3,2},{4,5},{5,4},{6,7},{7,6},{8,9},{9,8},{10,11... | collective-permute-start | bytes 393224 | tf_op jit(solution)/shard_map/ppermute | solution.py:51

commit v2 on v1

--- a/solution.py
+++ b/solution.py
@@ -347,7 +347,8 @@
     d0, d1, m2, p2 = lax.optimization_barrier((d0, d1, m2, p2))
     lo, hi = backward(0, bwd, boffs, tiles, d0, d1)
     s_lo, s_hi, w2 = lax.optimization_barrier((s_lo, s_hi, w2))
-    w = ring_sum(w, w2, s_hi[8 * B :], s_lo[8 * B :])
+    w = ring_sum(w, w2, s_hi[8 * B :], s_lo[8 * B :], F32)
+    w = (w + send(w, YN)).astype(BF16)
     s_lo, s_hi = blocks(s_lo[: 8 * B]), blocks(s_hi[: 8 * B])
     def spread(own, s, t, extra):
         near, down, up, two = (plus(own[k : k + 2], s[k : k + 2], t[k : k + 2]) for k in (0, 2, 4, 6))
@@ -358,10 +359,8 @@
     far, *rest = spread(hi, s_hi, t_hi, w)
     near, *parts = spread(lo, s_lo, t_lo, None)
     far = plus(far, *(blocks(r[: 2 * B]) for r in rest))
-    w = ring_sum(w, *(r[2 * B :] for r in rest))
-    other = send(carry(far, w), YN)
-    w = w.astype(F32) + other[2 * B :].astype(F32)
-    other = blocks(other[: 2 * B])
+    w = ring_sum(w, *(r[2 * B :] for r in rest), F32)
+    other = send(far, YN)
     got = send(w, CC)
     total = sum((t.astype(F32) for t in (near, *parts, other)), jnp.zeros((), F32))
     feature_grad = jnp.swapaxes(total, 1, 2).astype(BF16).reshape(2 * B, B)

time: 170 us -> 164 us (0.965)
  the two profiles are of different devices: /device:TPU:0 before, /device:TPU:48 now
where the time goes in v2:
time: 164 us; the launch traced here: 165 us
  waiting for transfers between devices  63.3 us (39%)
  Pallas kernels  50.5 us (31%)
  starting transfers between devices  43.4 us (26%)
  other arithmetic  3.5 us (2%)
  local copies, waits for them, and re-layouts  2.39 us (1%)
    ppermute x34, waiting for transfers between devices, send(): return lax.ppermute(value, AXES, pairs)  63.3 us
    ppermute x34, starting transfers between devices, send(): return lax.ppermute(value, AXES, pairs)  43.4 us
    pallas_call x4, Pallas kernels, forward(): pl.pallas_call(functools.partial(_forward_kernel, chunk), name=f'tiles_fo...  27.6 us
    pallas_call x4, Pallas kernels, backward(): pl.pallas_call(functools.partial(_backward_kernel, chunk, len(adds)), nam...  21.5 us
  transfers between devices with their start and end apart: 34, of which 17 were waited for; matrix products, arithmetic and copies ran while one was open for 2% of the time, Pallas kernels for 23%

profile of v2, /device:TPU:48, one launch (start us, length us, event | category | flops | bytes accessed | tf_op | source)
XLA Modules:
  0.0 164.7 jit_solution(8709112748815172004)
XLA Ops:
  0.7 1.2 copy-done
  1.9 1.4 collective-permute-start.5
  3.2 3.0 %collective-permute-start.2 = (bf16[2,256,256]{2,1,0:T(8,128)(2,1)S(1)}, bf16[2,256,256]{2,1,0:T(8,128)(2,1)S(1)}, u32[]{:S(2)}, u32[]{:S(2)}) collective-permute-start(bf16[2,256,256]{2,1,0:T(8,128)(2,1)S(1)} %constant_dynamic-slice_fusion), channel_id=1, source_target_pairs={{0,8},{1,65},{2,10},{3,67},{4,12},{5,69},{6,14},{7,71},{8,0},{9,73... | collective-permute-start | bytes 786440 | tf_op jit(solution)/shard_map/ppermute | solution.py:51
  6.3 1.1 collective-permute-start.1
  7.4 0.9 collective-permute-start
  8.3 1.7 %collective-permute-done.5 = bf16[2,256,256]{2,1,0:T(8,128)(2,1)S(1)} collective-permute-done((bf16[2,256,256]{2,1,0:T(8,128)(2,1)S(1)}, bf16[2,256,256]{2,1,0:T(8,128)(2,1)S(1)}, u32[]{:S(2)}, u32[]{:S(2)}) %collective-permute-start.5) | collective-permute-done | bytes 262176 | tf_op jit(solution)/shard_map/ppermute | solution.py:51
  10.0 3.0 %collective-permute-start.8 = (bf16[2,256,256]{2,1,0:T(8,128)(2,1)S(1)}, bf16[2,256,256]{2,1,0:T(8,128)(2,1)S(1)}, u32[]{:S(2)}, u32[]{:S(2)}) collective-permute-start(bf16[2,256,256]{2,1,0:T(8,128)(2,1)S(1)} %collective-permute-done.5), channel_id=1, source_target_pairs={{0,8},{1,65},{2,10},{3,67},{4,12},{5,69},{6,14},{7,71},{8,0},{9,73... | collective-permute-start | bytes 786440 | tf_op jit(solution)/shard_map/ppermute | solution.py:51
  13.0 1.1 collective-permute-start.7
  14.2 0.9 collective-permute-start.6
  15.7 2.1 %collective-permute-done.8 = bf16[2,256,256]{2,1,0:T(8,128)(2,1)S(1)} collective-permute-done((bf16[2,256,256]{2,1,0:T(8,128)(2,1)S(1)}, bf16[2,256,256]{2,1,0:T(8,128)(2,1)S(1)}, u32[]{:S(2)}, u32[]{:S(2)}) %collective-permute-start.8) | collective-permute-done | bytes 262176 | tf_op jit(solution)/shard_map/ppermute | solution.py:51
  17.9 1.9 %collective-permute-start.3 = (bf16[8,256,256]{2,1,0:T(8,128)(2,1)S(1)}, bf16[8,256,256]{2,1,0:T(8,128)(2,1)}, u32[]{:S(2)}, u32[]{:S(2)}) collective-permute-start(bf16[8,256,256]{2,1,0:T(8,128)(2,1)S(1)} %pad_maximum_fusion.fa), channel_id=1, source_target_pairs={{0,32},{1,5},{2,34},{3,7},{4,36},{5,9},{6,38},{7,11},{8,40},{9,13}... | collective-permute-start | bytes 3145736 | tf_op jit(solution)/shard_map/ppermute | solution.py:51
  19.8 5.7 %collective-permute-done.7 = bf16[2,256,256]{2,1,0:T(8,128)(2,1)S(1)} collective-permute-done((bf16[2,256,256]{2,1,0:T(8,128)(2,1)S(1)}, bf16[2,256,256]{2,1,0:T(8,128)(2,1)S(1)}, u32[]{:S(2)}, u32[]{:S(2)}) %collective-permute-start.7) | collective-permute-done | bytes 262176 | tf_op jit(solution)/shard_map/ppermute | solution.py:51
  25.8 2.6 %collective-permute-start.11 = (bf16[8,256,256]{2,1,0:T(8,128)(2,1)S(1)}, bf16[8,256,256]{2,1,0:T(8,128)(2,1)}, u32[]{:S(2)}, u32[]{:S(2)}) collective-permute-start(bf16[8,256,256]{2,1,0:T(8,128)(2,1)S(1)} %pad_maximum_fusion.1.fb), channel_id=1, source_target_pairs={{0,32},{1,5},{2,34},{3,7},{4,36},{5,9},{6,38},{7,11},{8,40},{9,13}... | collective-permute-start | bytes 3145736 | tf_op jit(solution)/shard_map/ppermute | solution.py:51
  29.5 5.7 %tiles_forward_0.1.refs_0_ = f32[8,256,256]{2,1,0:T(8,128)S(1)} custom-call(s32[160]{0:T(256)S(1)} %select_reduce_fusion.1.tab, s32[9]{0:T(128)S(1)} %convert_reduce_fusion.3.offs, bf16[160,256,256]{2,1,0:T(8,128)(2,1)} %bitcast.46, bf16[8,256,256]{2,1,0:T(8,128)(2,1)S(1)} %pad_maximum_fusion.fa, bf16[8,256,256]{2,1,0:T(8,128)(2,1)S(1)} %pad_maximum_fusion.1.fb), custom_call_target="tpu_custom_call" | custom-call | flops 16777216 | bytes 65536 | tf_op jit(solution)/shard_map/tiles_forward_0/pallas_call | solution.py:174
  35.3 1.9 %collective-permute-start.10 = (bf16[8,256,256]{2,1,0:T(8,128)(2,1)}, bf16[8,256,256]{2,1,0:T(8,128)(2,1)S(1)}, u32[]{:S(2)}, u32[]{:S(2)}) collective-permute-start(bf16[8,256,256]{2,1,0:T(8,128)(2,1)} %collective-permute-done.3.fa), channel_id=1, source_target_pairs={{0,32},{1,5},{2,34},{3,7},{4,36},{5,9},{6,38},{7,11},{8,40},{9,13}... | collective-permute-start | bytes 3145736 | tf_op jit(solution)/shard_map/ppermute | solution.py:51
  37.2 8.3 %tiles_forward_1.1.refs_0_ = f32[8,256,256]{2,1,0:T(8,128)S(1)} custom-call(s32[160]{0:T(256)S(1)} %select_reduce_fusion.1.tab, s32[9]{0:T(128)S(1)} %convert_reduce_fusion.3.offs, bf16[160,256,256]{2,1,0:T(8,128)(2,1)} %bitcast.47, bf16[8,256,256]{2,1,0:T(8,128)(2,1)} %collective-permute-done.3.fa, ...), custom_call_target="tpu_custom_call", output_to_operand_aliasing={{}: (5, {})} | custom-call | flops 16777216 | bytes 65536 | tf_op jit(solution)/shard_map/tiles_forward_1/pallas_call | solution.py:174
  45.6 1.6 collective-permute-start.13
  47.1 7.0 %tiles_forward_2.1.refs_0_ = f32[8,256,256]{2,1,0:T(8,128)S(1)} custom-call(s32[160]{0:T(256)S(1)} %select_reduce_fusion.1.tab, s32[9]{0:T(128)S(1)} %convert_reduce_fusion.3.offs, bf16[160,256,256]{2,1,0:T(8,128)(2,1)} %bitcast.48, bf16[8,256,256]{2,1,0:T(8,128)(2,1)} %collective-permute-done.11.fa, ...), custom_call_target="tpu_custom_call", output_to_operand_aliasing={{}: (5, {})} | custom-call | flops 16777216 | bytes 65536 | tf_op jit(solution)/shard_map/tiles_forward_2/pallas_call | solution.py:174
  54.1 1.0 collective-permute-done.10.fa
  55.2 5.5 %collective-permute-done.13.fb = bf16[8,256,256]{2,1,0:T(8,128)(2,1)S(1)} collective-permute-done((bf16[8,256,256]{2,1,0:T(8,128)(2,1)}, bf16[8,256,256]{2,1,0:T(8,128)(2,1)S(1)}, u32[]{:S(2)}, u32[]{:S(2)}) %collective-permute-start.13) | collective-permute-done | bytes 1048608 | tf_op jit(solution)/shard_map/ppermute | solution.py:51
  60.7 6.5 %tiles_forward_3.1 = f32[8,256,256]{2,1,0:T(8,128)S(1)} custom-call(s32[160]{0:T(256)S(1)} %select_reduce_fusion.1.tab, s32[9]{0:T(128)S(1)} %convert_reduce_fusion.3.offs, bf16[160,256,256]{2,1,0:T(8,128)(2,1)} %bitcast.49, bf16[8,256,256]{2,1,0:T(8,128)(2,1)S(1)} %collective-permute-done.10.fa, ...), custom_call_target="tpu_custom_call", output_to_operand_aliasing={{}: (5, {})} | custom-call | flops 16777216 | bytes 65536 | tf_op jit(solution)/shard_map/tiles_forward_3/pallas_call | solution.py:174
  67.4 2.6 %collective-permute-done.14 = f32[4,256,256]{2,1,0:T(8,128)S(1)} collective-permute-done((f32[4,256,256]{2,1,0:T(8,128)S(1)}, f32[4,256,256]{2,1,0:T(8,128)S(1)}, u32[]{:S(2)}, u32[]{:S(2)}) %collective-permute-start.14) | collective-permute-done | bytes 1048608 | tf_op jit(solution)/shard_map/ppermute | solution.py:51
  70.3 1.4 collective-permute-start.15
  71.9 13.9 %collective-permute-done.15.far = bf16[4,256,256]{2,1,0:T(8,128)(2,1)S(1)} collective-permute-done((bf16[4,256,256]{2,1,0:T(8,128)(2,1)S(1)}, bf16[4,256,256]{2,1,0:T(8,128)(2,1)S(1)}, u32[]{:S(2)}, u32[]{:S(2)}) %collective-permute-start.15) | collective-permute-done | bytes 524320 | tf_op jit(solution)/shard_map/ppermute | solution.py:51
  85.8 1.4 dense.1
  88.1 1.2 collective-permute-done.17
  89.3 5.3 %tiles_backward_3.1 = (bf16[8,256,256]{2,1,0:T(8,128)(2,1)S(1)}, bf16[8,256,256]{2,1,0:T(8,128)(2,1)S(1)}) custom-call(s32[160]{0:T(256)S(1)} %select_reduce_fusion.tab, s32[9]{0:T(128)S(1)} %convert_reduce_fusion.2.offs, bf16[160,256,256]{2,1,0:T(8,128)(2,1)} %bitcast.50, bf16[4,256,256]{2,1,0:T(8,128)(2,1)S(1)} %get-tuple-element.64.d0, ...), custom_call_target="tpu_custom_call" | custom-call | flops 16777216 | bytes 65536 | tf_op jit(solution)/shard_map/tiles_backward_3/pallas_call | solution.py:223
  94.7 2.1 %collective-permute-start.18 = (bf16[8,256,256]{2,1,0:T(8,128)(2,1)S(1)}, bf16[8,256,256]{2,1,0:T(8,128)(2,1)S(1)}, u32[]{:S(2)}, u32[]{:S(2)}) collective-permute-start(bf16[8,256,256]{2,1,0:T(8,128)(2,1)S(1)} %get-tuple-element.50), channel_id=1, source_target_pairs={{0,32},{1,5},{2,34},{3,7},{4,36},{5,9},{6,38},{7,11},{8,40},{9,13}... | collective-permute-start | bytes 3145736 | tf_op jit(solution)/shard_map/ppermute | solution.py:51
  96.8 5.7 %tiles_backward_1.1 = (bf16[2176,256]{1,0:T(8,128)(2,1)S(1)}, bf16[2176,256]{1,0:T(8,128)(2,1)S(1)}) custom-call(s32[160]{0:T(256)S(1)} %select_reduce_fusion.tab, s32[9]{0:T(128)S(1)} %convert_reduce_fusion.2.offs, bf16[160,256,256]{2,1,0:T(8,128)(2,1)} %bitcast.51, bf16[4,256,256]{2,1,0:T(8,128)(2,1)S(1)} %get-tuple-element.64.d0, ...), custom_call_target="tpu_custom_call" | custom-call | flops 16777216 | bytes 65536 | tf_op jit(solution)/shard_map/tiles_backward_1/pallas_call | solution.py:223
  102.4 2.3 %collective-permute-start.20 = (bf16[2176,256]{1,0:T(8,128)(2,1)S(1)}, bf16[2176,256]{1,0:T(8,128)(2,1)S(1)}, u32[]{:S(2)}, u32[]{:S(2)}) collective-permute-start(bf16[2176,256]{1,0:T(8,128)(2,1)S(1)} %get-tuple-element.56), channel_id=1, source_target_pairs={{0,96},{1,13},{2,98},{3,15},{4,100},{5,1},{6,102},{7,3},{8,104},{9... | collective-permute-start | bytes 3342344 | tf_op jit(solution)/shard_map/ppermute | solution.py:51
  104.7 4.8 %collective-permute-done.18.refs_1_ = bf16[8,256,256]{2,1,0:T(8,128)(2,1)S(1)} collective-permute-done((bf16[8,256,256]{2,1,0:T(8,128)(2,1)S(1)}, bf16[8,256,256]{2,1,0:T(8,128)(2,1)S(1)}, u32[]{:S(2)}, u32[]{:S(2)}) %collective-permute-start.18) | collective-permute-done | bytes 1048608 | tf_op jit(solution)/shard_map/ppermute | solution.py:51
  109.5 3.1 %collective-permute-done.19.refs_0_ = bf16[8,256,256]{2,1,0:T(8,128)(2,1)S(1)} collective-permute-done((bf16[8,256,256]{2,1,0:T(8,128)(2,1)S(1)}, bf16[8,256,256]{2,1,0:T(8,128)(2,1)S(1)}, u32[]{:S(2)}, u32[]{:S(2)}) %collective-permute-start.19) | collective-permute-done | bytes 1048608 | tf_op jit(solution)/shard_map/ppermute | solution.py:51
  112.6 5.2 %tiles_backward_2.1 = (bf16[8,256,256]{2,1,0:T(8,128)(2,1)S(1)}, bf16[8,256,256]{2,1,0:T(8,128)(2,1)S(1)}) custom-call(s32[160]{0:T(256)S(1)} %select_reduce_fusion.tab, s32[9]{0:T(128)S(1)} %convert_reduce_fusion.2.offs, bf16[160,256,256]{2,1,0:T(8,128)(2,1)} %bitcast.52, bf16[4,256,256]{2,1,0:T(8,128)(2,1)S(1)} %get-tuple-element.64.d0, ...), custom_call_target="tpu_custom_call" | custom-call | flops 16777216 | bytes 65536 | tf_op jit(solution)/shard_map/tiles_backward_2/pallas_call | solution.py:223
  118.0 3.4 %collective-permute-start.22 = (bf16[128,256]{1,0:T(8,128)(2,1)S(1)}, bf16[128,256]{1,0:T(8,128)(2,1)S(1)}, u32[]{:S(2)}, u32[]{:S(2)}) collective-permute-start(bf16[128,256]{1,0:T(8,128)(2,1)S(1)} %fusion.20.refs_0_), channel_id=1, source_target_pairs={{0,64},{1,9},{2,66},{3,11},{4,68},{5,13},{6,70},{7,15},{8,72},{9,1... | collective-permute-start | bytes 196616 | tf_op jit(solution)/shard_map/ppermute | solution.py:51
  121.4 2.5 %collective-permute-start.23 = (bf16[8,256,256]{2,1,0:T(8,128)(2,1)S(1)}, bf16[8,256,256]{2,1,0:T(8,128)(2,1)S(1)}, u32[]{:S(2)}, u32[]{:S(2)}) collective-permute-start(bf16[8,256,256]{2,1,0:T(8,128)(2,1)S(1)} %get-tuple-element.63), channel_id=1, source_target_pairs={{0,32},{1,5},{2,34},{3,7},{4,36},{5,9},{6,38},{7,11},{8,40},{9,13}... | collective-permute-start | bytes 3145736 | tf_op jit(solution)/shard_map/ppermute | solution.py:51
  123.9 5.3 %tiles_backward_0.1 = (bf16[8,256,256]{2,1,0:T(8,128)(2,1)S(1)}, bf16[8,256,256]{2,1,0:T(8,128)(2,1)S(1)}) custom-call(s32[160]{0:T(256)S(1)} %select_reduce_fusion.tab, s32[9]{0:T(128)S(1)} %convert_reduce_fusion.2.offs, bf16[160,256,256]{2,1,0:T(8,128)(2,1)} %bitcast.53, bf16[4,256,256]{2,1,0:T(8,128)(2,1)S(1)} %get-tuple-element.64.d0, ...), custom_call_target="tpu_custom_call" | custom-call | flops 16777216 | bytes 65536 | tf_op jit(solution)/shard_map/tiles_backward_0/pallas_call | solution.py:223
  129.3 8.7 %collective-permute-done.22 = bf16[128,256]{1,0:T(8,128)(2,1)S(1)} collective-permute-done((bf16[128,256]{1,0:T(8,128)(2,1)S(1)}, bf16[128,256]{1,0:T(8,128)(2,1)S(1)}, u32[]{:S(2)}, u32[]{:S(2)}) %collective-permute-start.22) | collective-permute-done | bytes 65568 | tf_op jit(solution)/shard_map/ppermute | solution.py:51
  138.0 1.0 collective-permute-start.28
  139.1 4.0 %collective-permute-done.28 = f32[128,256]{1,0:T(8,128)S(1)} collective-permute-done((f32[128,256]{1,0:T(8,128)S(1)}, f32[128,256]{1,0:T(8,128)S(1)}, u32[]{:S(2)}, u32[]{:S(2)}) %collective-permute-start.28) | collective-permute-done | bytes 131104 | tf_op jit(solution)/shard_map/ppermute | solution.py:51
  143.6 4.7 %collective-permute-start.30 = (bf16[640,256]{1,0:T(8,128)(2,1)S(1)}, bf16[640,256]{1,0:T(8,128)(2,1)S(1)}, u32[]{:S(2)}, u32[]{:S(2)}) collective-permute-start(bf16[640,256]{1,0:T(8,128)(2,1)S(1)} %get-tuple-element.96), channel_id=1, source_target_pairs={{0,4},{1,33},{2,6},{3,35},{4,8},{5,37},{6,10},{7,39},{8,12},{9,41}... | collective-permute-start | bytes 983048 | tf_op jit(solution)/shard_map/ppermute | solution.py:51
  148.6 2.1 %collective-permute-start.24 = (bf16[2,256,256]{2,1,0:T(8,128)(2,1)S(1)}, bf16[2,256,256]{2,1,0:T(8,128)(2,1)S(1)}, u32[]{:S(2)}, u32[]{:S(2)}) collective-permute-start(bf16[2,256,256]{2,1,0:T(8,128)(2,1)S(1)} %get-tuple-element.81), channel_id=1, source_target_pairs={{0,8},{1,65},{2,10},{3,67},{4,12},{5,69},{6,14},{7,71},{8,0},{9,73... | collective-permute-start | bytes 786440 | tf_op jit(solution)/shard_map/ppermute | solution.py:51
  150.8 2.6 %collective-permute-start.26 = (bf16[2,256,256]{2,1,0:T(8,128)(2,1)S(1)}, bf16[2,256,256]{2,1,0:T(8,128)(2,1)S(1)}, u32[]{:S(2)}, u32[]{:S(2)}) collective-permute-start(bf16[2,256,256]{2,1,0:T(8,128)(2,1)S(1)} %get-tuple-element.82), channel_id=1, source_target_pairs={{0,12},{1,97},{2,14},{3,99},{4,0},{5,101},{6,2},{7,103},{8,4},{9,1... | collective-permute-start | bytes 786440 | tf_op jit(solution)/shard_map/ppermute | solution.py:51
  153.5 2.2 %collective-permute-done.30 = bf16[640,256]{1,0:T(8,128)(2,1)S(1)} collective-permute-done((bf16[640,256]{1,0:T(8,128)(2,1)S(1)}, bf16[640,256]{1,0:T(8,128)(2,1)S(1)}, u32[]{:S(2)}, u32[]{:S(2)}) %collective-permute-start.30) | collective-permute-done | bytes 327712 | tf_op jit(solution)/shard_map/ppermute | solution.py:51
  155.7 1.2 collective-permute-done.31
  157.5 1.3 collective-permute-done.33
  159.6 3.0 %collective-permute-done.26 = bf16[2,256,256]{2,1,0:T(8,128)(2,1)S(1)} collective-permute-done((bf16[2,256,256]{2,1,0:T(8,128)(2,1)S(1)}, bf16[2,256,256]{2,1,0:T(8,128)(2,1)S(1)}, u32[]{:S(2)}, u32[]{:S(2)}) %collective-permute-start.26) | collective-permute-done | bytes 262176 | tf_op jit(solution)/shard_map/ppermute | solution.py:51
  162.6 1.0 collective-permute-done.32
  163.8 0.8 copy.14
  (70 shorter events, 5.7 us)
Async XLA Ops:
  0.6 1.2 copy-start
  1.9 8.1 %collective-permute-start.5 = (bf16[2,256,256]{2,1,0:T(8,128)(2,1)S(1)}, bf16[2,256,256]{2,1,0:T(8,128)(2,1)S(1)}, u32[]{:S(2)}, u32[]{:S(2)}) collective-permute-start(bf16[2,256,256]{2,1,0:T(8,128)(2,1)S(1)} %constant_dynamic-slice_fusion), channel_id=1, source_target_pairs={{0,16},{1,17},{2,18},{3,19},{4,20},{5,21},{6,22},{7,23},{8,24},{9,... | collective-permute-start | bytes 786440 | tf_op jit(solution)/shard_map/ppermute | solution.py:51
  3.2 10.9 %collective-permute-start.2 = (bf16[2,256,256]{2,1,0:T(8,128)(2,1)S(1)}, bf16[2,256,256]{2,1,0:T(8,128)(2,1)S(1)}, u32[]{:S(2)}, u32[]{:S(2)}) collective-permute-start(bf16[2,256,256]{2,1,0:T(8,128)(2,1)S(1)} %constant_dynamic-slice_fusion), channel_id=1, source_target_pairs={{0,8},{1,65},{2,10},{3,67},{4,12},{5,69},{6,14},{7,71},{8,0},{9,73... | collective-permute-start | bytes 786440 | tf_op jit(solution)/shard_map/ppermute | solution.py:51
  6.3 8.8 %collective-permute-start.1 = (bf16[2,256,256]{2,1,0:T(8,128)(2,1)S(1)}, bf16[2,256,256]{2,1,0:T(8,128)(2,1)S(1)}, u32[]{:S(2)}, u32[]{:S(2)}) collective-permute-start(bf16[2,256,256]{2,1,0:T(8,128)(2,1)S(1)} %constant_dynamic-slice_fusion), channel_id=1, source_target_pairs={{0,12},{1,97},{2,14},{3,99},{4,0},{5,101},{6,2},{7,103},{8,4},{9,1... | collective-permute-start | bytes 786440 | tf_op jit(solution)/shard_map/ppermute | solution.py:51
  7.4 8.0 %collective-permute-start = (bf16[2,256,256]{2,1,0:T(8,128)(2,1)S(1)}, bf16[2,256,256]{2,1,0:T(8,128)(2,1)S(1)}, u32[]{:S(2)}, u32[]{:S(2)}) collective-permute-start(bf16[2,256,256]{2,1,0:T(8,128)(2,1)S(1)} %constant_dynamic-slice_fusion), channel_id=1, source_target_pairs={{0,4},{1,33},{2,6},{3,35},{4,8},{5,37},{6,10},{7,39},{8,12},{9,41}... | collective-permute-start | bytes 786440 | tf_op jit(solution)/shard_map/ppermute | solution.py:51
  10.0 7.9 %collective-permute-start.8 = (bf16[2,256,256]{2,1,0:T(8,128)(2,1)S(1)}, bf16[2,256,256]{2,1,0:T(8,128)(2,1)S(1)}, u32[]{:S(2)}, u32[]{:S(2)}) collective-permute-start(bf16[2,256,256]{2,1,0:T(8,128)(2,1)S(1)} %collective-permute-done.5), channel_id=1, source_target_pairs={{0,8},{1,65},{2,10},{3,67},{4,12},{5,69},{6,14},{7,71},{8,0},{9,73... | collective-permute-start | bytes 786440 | tf_op jit(solution)/shard_map/ppermute | solution.py:51
  13.0 12.5 %collective-permute-start.7 = (bf16[2,256,256]{2,1,0:T(8,128)(2,1)S(1)}, bf16[2,256,256]{2,1,0:T(8,128)(2,1)S(1)}, u32[]{:S(2)}, u32[]{:S(2)}) collective-permute-start(bf16[2,256,256]{2,1,0:T(8,128)(2,1)S(1)} %collective-permute-done.5), channel_id=1, source_target_pairs={{0,12},{1,97},{2,14},{3,99},{4,0},{5,101},{6,2},{7,103},{8,4},{9,1... | collective-permute-start | bytes 786440 | tf_op jit(solution)/shard_map/ppermute | solution.py:51
  14.2 11.3 %collective-permute-start.6 = (bf16[2,256,256]{2,1,0:T(8,128)(2,1)S(1)}, bf16[2,256,256]{2,1,0:T(8,128)(2,1)S(1)}, u32[]{:S(2)}, u32[]{:S(2)}) collective-permute-start(bf16[2,256,256]{2,1,0:T(8,128)(2,1)S(1)} %collective-permute-done.5), channel_id=1, source_target_pairs={{0,4},{1,33},{2,6},{3,35},{4,8},{5,37},{6,10},{7,39},{8,12},{9,41}... | collective-permute-start | bytes 786440 | tf_op jit(solution)/shard_map/ppermute | solution.py:51
  15.1 10.6 %collective-permute-start.9 = (bf16[2,256,256]{2,1,0:T(8,128)(2,1)}, bf16[2,256,256]{2,1,0:T(8,128)(2,1)S(1)}, u32[]{:S(2)}, u32[]{:S(2)}) collective-permute-start(bf16[2,256,256]{2,1,0:T(8,128)(2,1)} %bitcast.44), channel_id=1, source_target_pairs={{0,2},{1,3},{2,0},{3,1},{4,6},{5,7},{6,4},{7,5},{8,10},{9,11},{10,... | collective-permute-start | bytes 786440 | tf_op jit(solution)/shard_map/ppermute | solution.py:51
  15.5 13.4 %copy-start.3 = (s32[1,1,160]{2,1,0:T(1,128)S(1)}, s32[1,1,160]{2,1,0:T(1,128)}, u32[]{:S(2)}) copy-start(s32[1,1,160]{2,1,0:T(1,128)} %param.12) | copy-start | bytes 1924
  15.6 13.5 %copy-start.4 = (s32[1,1,160]{2,1,0:T(1,128)S(1)}, s32[1,1,160]{2,1,0:T(1,128)}, u32[]{:S(2)}) copy-start(s32[1,1,160]{2,1,0:T(1,128)} %param.11) | copy-start | bytes 1924
  15.6 19.7 %collective-permute-start.4 = (bf16[8,256,256]{2,1,0:T(8,128)(2,1)S(1)}, bf16[8,256,256]{2,1,0:T(8,128)(2,1)}, u32[]{:S(2)}, u32[]{:S(2)}) collective-permute-start(bf16[8,256,256]{2,1,0:T(8,128)(2,1)S(1)} %pad_maximum_fusion.fa), channel_id=1, source_target_pairs={{0,96},{1,13},{2,98},{3,15},{4,100},{5,1},{6,102},{7,3},{8,104},{9... | collective-permute-start | bytes 3145736 | tf_op jit(solution)/shard_map/ppermute | solution.py:51
  17.9 17.4 %collective-permute-start.3 = (bf16[8,256,256]{2,1,0:T(8,128)(2,1)S(1)}, bf16[8,256,256]{2,1,0:T(8,128)(2,1)}, u32[]{:S(2)}, u32[]{:S(2)}) collective-permute-start(bf16[8,256,256]{2,1,0:T(8,128)(2,1)S(1)} %pad_maximum_fusion.fa), channel_id=1, source_target_pairs={{0,32},{1,5},{2,34},{3,7},{4,36},{5,9},{6,38},{7,11},{8,40},{9,13}... | collective-permute-start | bytes 3145736 | tf_op jit(solution)/shard_map/ppermute | solution.py:51
  25.7 19.9 %collective-permute-start.12 = (bf16[8,256,256]{2,1,0:T(8,128)(2,1)S(1)}, bf16[8,256,256]{2,1,0:T(8,128)(2,1)}, u32[]{:S(2)}, u32[]{:S(2)}) collective-permute-start(bf16[8,256,256]{2,1,0:T(8,128)(2,1)S(1)} %pad_maximum_fusion.1.fb), channel_id=1, source_target_pairs={{0,96},{1,13},{2,98},{3,15},{4,100},{5,1},{6,102},{7,3},{8,104},{9... | collective-permute-start | bytes 3145736 | tf_op jit(solution)/shard_map/ppermute | solution.py:51
  25.8 19.8 %collective-permute-start.11 = (bf16[8,256,256]{2,1,0:T(8,128)(2,1)S(1)}, bf16[8,256,256]{2,1,0:T(8,128)(2,1)}, u32[]{:S(2)}, u32[]{:S(2)}) collective-permute-start(bf16[8,256,256]{2,1,0:T(8,128)(2,1)S(1)} %pad_maximum_fusion.1.fb), channel_id=1, source_target_pairs={{0,32},{1,5},{2,34},{3,7},{4,36},{5,9},{6,38},{7,11},{8,40},{9,13}... | collective-permute-start | bytes 3145736 | tf_op jit(solution)/shard_map/ppermute | solution.py:51
  35.3 19.8 %collective-permute-start.10 = (bf16[8,256,256]{2,1,0:T(8,128)(2,1)}, bf16[8,256,256]{2,1,0:T(8,128)(2,1)S(1)}, u32[]{:S(2)}, u32[]{:S(2)}) collective-permute-start(bf16[8,256,256]{2,1,0:T(8,128)(2,1)} %collective-permute-done.3.fa), channel_id=1, source_target_pairs={{0,32},{1,5},{2,34},{3,7},{4,36},{5,9},{6,38},{7,11},{8,40},{9,13}... | collective-permute-start | bytes 3145736 | tf_op jit(solution)/shard_map/ppermute | solution.py:51
  45.6 15.1 %collective-permute-start.13 = (bf16[8,256,256]{2,1,0:T(8,128)(2,1)}, bf16[8,256,256]{2,1,0:T(8,128)(2,1)S(1)}, u32[]{:S(2)}, u32[]{:S(2)}) collective-permute-start(bf16[8,256,256]{2,1,0:T(8,128)(2,1)} %collective-permute-done.12.fb), channel_id=1, source_target_pairs={{0,96},{1,13},{2,98},{3,15},{4,100},{5,1},{6,102},{7,3},{8,104},{9... | collective-permute-start | bytes 3145736 | tf_op jit(solution)/shard_map/ppermute | solution.py:51
  67.3 18.6 %copy-start.1 = (bf16[512,256]{1,0:T(8,128)(2,1)S(1)}, bf16[512,256]{1,0:T(8,128)(2,1)}, u32[]{:S(2)}) copy-start(bf16[512,256]{1,0:T(8,128)(2,1)} %param.9) | copy-start | bytes 786436
  67.3 18.5 %copy-start.2 = (bf16[256,256]{1,0:T(8,128)(2,1)S(1)}, bf16[256,256]{1,0:T(8,128)(2,1)}, u32[]{:S(2)}) copy-start(bf16[256,256]{1,0:T(8,128)(2,1)} %w_ref.1) | copy-start | bytes 393220
  67.3 2.7 %collective-permute-start.14 = (f32[4,256,256]{2,1,0:T(8,128)S(1)}, f32[4,256,256]{2,1,0:T(8,128)S(1)}, u32[]{:S(2)}, u32[]{:S(2)}) collective-permute-start(f32[4,256,256]{2,1,0:T(8,128)S(1)} %slice.163), channel_id=1, source_target_pairs={{0,1},{1,0},{2,3},{3,2},{4,5},{5,4},{6,7},{7,6},{8,9},{9,8},{10,11... | collective-permute-start | bytes 3145736 | tf_op jit(solution)/shard_map/ppermute | solution.py:51
  70.3 15.5 %collective-permute-start.15 = (bf16[4,256,256]{2,1,0:T(8,128)(2,1)S(1)}, bf16[4,256,256]{2,1,0:T(8,128)(2,1)S(1)}, u32[]{:S(2)}, u32[]{:S(2)}) collective-permute-start(bf16[4,256,256]{2,1,0:T(8,128)(2,1)S(1)} %fusion.near), channel_id=1, source_target_pairs={{0,2},{1,3},{2,0},{3,1},{4,6},{5,7},{6,4},{7,5},{8,10},{9,11},{10,... | collective-permute-start | bytes 1572872 | tf_op jit(solution)/shard_map/ppermute | solution.py:51
  87.2 2.1 %collective-permute-start.16 = (bf16[4,256,256]{2,1,0:T(8,128)(2,1)S(1)}, bf16[4,256,256]{2,1,0:T(8,128)(2,1)S(1)}, u32[]{:S(2)}, u32[]{:S(2)}) collective-permute-start(bf16[4,256,256]{2,1,0:T(8,128)(2,1)S(1)} %get-tuple-element.64.d0), channel_id=1, source_target_pairs={{0,1},{1,0},{2,3},{3,2},{4,5},{5,4},{6,7},{7,6},{8,9},{9,8},{10,11... | collective-permute-start | bytes 1572872 | tf_op jit(solution)/shard_map/ppermute | solution.py:51
  87.3 2.0 %collective-permute-start.17 = (f32[128,256]{1,0:T(8,128)S(1)}, f32[128,256]{1,0:T(8,128)S(1)}, u32[]{:S(2)}, u32[]{:S(2)}) collective-permute-start(f32[128,256]{1,0:T(8,128)S(1)} %dynamic-slice_bitcast_fusion), channel_id=1, source_target_pairs={{0,1},{1,0},{2,3},{3,2},{4,5},{5,4},{6,7},{7,6},{8,9},{9,8},{10,11... | collective-permute-start | bytes 393224 | tf_op jit(solution)/shard_map/ppermute | solution.py:51
  94.7 14.9 %collective-permute-start.18 = (bf16[8,256,256]{2,1,0:T(8,128)(2,1)S(1)}, bf16[8,256,256]{2,1,0:T(8,128)(2,1)S(1)}, u32[]{:S(2)}, u32[]{:S(2)}) collective-permute-start(bf16[8,256,256]{2,1,0:T(8,128)(2,1)S(1)} %get-tuple-element.50), channel_id=1, source_target_pairs={{0,32},{1,5},{2,34},{3,7},{4,36},{5,9},{6,38},{7,11},{8,40},{9,13}... | collective-permute-start | bytes 3145736 | tf_op jit(solution)/shard_map/ppermute | solution.py:51
  96.7 15.9 %collective-permute-start.19 = (bf16[8,256,256]{2,1,0:T(8,128)(2,1)S(1)}, bf16[8,256,256]{2,1,0:T(8,128)(2,1)S(1)}, u32[]{:S(2)}, u32[]{:S(2)}) collective-permute-start(bf16[8,256,256]{2,1,0:T(8,128)(2,1)S(1)} %get-tuple-element.51), channel_id=1, source_target_pairs={{0,96},{1,13},{2,98},{3,15},{4,100},{5,1},{6,102},{7,3},{8,104},{9... | collective-permute-start | bytes 3145736 | tf_op jit(solution)/shard_map/ppermute | solution.py:51
  102.4 35.5 %collective-permute-start.20 = (bf16[2176,256]{1,0:T(8,128)(2,1)S(1)}, bf16[2176,256]{1,0:T(8,128)(2,1)S(1)}, u32[]{:S(2)}, u32[]{:S(2)}) collective-permute-start(bf16[2176,256]{1,0:T(8,128)(2,1)S(1)} %get-tuple-element.56), channel_id=1, source_target_pairs={{0,96},{1,13},{2,98},{3,15},{4,100},{5,1},{6,102},{7,3},{8,104},{9... | collective-permute-start | bytes 3342344 | tf_op jit(solution)/shard_map/ppermute | solution.py:51
  104.7 33.3 %collective-permute-start.21 = (bf16[2176,256]{1,0:T(8,128)(2,1)S(1)}, bf16[2176,256]{1,0:T(8,128)(2,1)S(1)}, u32[]{:S(2)}, u32[]{:S(2)}) collective-permute-start(bf16[2176,256]{1,0:T(8,128)(2,1)S(1)} %get-tuple-element.57), channel_id=1, source_target_pairs={{0,32},{1,5},{2,34},{3,7},{4,36},{5,9},{6,38},{7,11},{8,40},{9,13}... | collective-permute-start | bytes 3342344 | tf_op jit(solution)/shard_map/ppermute | solution.py:51
  117.9 25.2 %collective-permute-start.27 = (bf16[8,256,256]{2,1,0:T(8,128)(2,1)S(1)}, bf16[8,256,256]{2,1,0:T(8,128)(2,1)S(1)}, u32[]{:S(2)}, u32[]{:S(2)}) collective-permute-start(bf16[8,256,256]{2,1,0:T(8,128)(2,1)S(1)} %get-tuple-element.62), channel_id=1, source_target_pairs={{0,96},{1,13},{2,98},{3,15},{4,100},{5,1},{6,102},{7,3},{8,104},{9... | collective-permute-start | bytes 3145736 | tf_op jit(solution)/shard_map/ppermute | solution.py:51
  118.0 20.0 %collective-permute-start.22 = (bf16[128,256]{1,0:T(8,128)(2,1)S(1)}, bf16[128,256]{1,0:T(8,128)(2,1)S(1)}, u32[]{:S(2)}, u32[]{:S(2)}) collective-permute-start(bf16[128,256]{1,0:T(8,128)(2,1)S(1)} %fusion.20.refs_0_), channel_id=1, source_target_pairs={{0,64},{1,9},{2,66},{3,11},{4,68},{5,13},{6,70},{7,15},{8,72},{9,1... | collective-permute-start | bytes 196616 | tf_op jit(solution)/shard_map/ppermute | solution.py:51
  121.4 26.9 %collective-permute-start.23 = (bf16[8,256,256]{2,1,0:T(8,128)(2,1)S(1)}, bf16[8,256,256]{2,1,0:T(8,128)(2,1)S(1)}, u32[]{:S(2)}, u32[]{:S(2)}) collective-permute-start(bf16[8,256,256]{2,1,0:T(8,128)(2,1)S(1)} %get-tuple-element.63), channel_id=1, source_target_pairs={{0,32},{1,5},{2,34},{3,7},{4,36},{5,9},{6,38},{7,11},{8,40},{9,13}... | collective-permute-start | bytes 3145736 | tf_op jit(solution)/shard_map/ppermute | solution.py:51
  138.0 5.0 %collective-permute-start.28 = (f32[128,256]{1,0:T(8,128)S(1)}, f32[128,256]{1,0:T(8,128)S(1)}, u32[]{:S(2)}, u32[]{:S(2)}) collective-permute-start(f32[128,256]{1,0:T(8,128)S(1)} %add_add_fusion.1), channel_id=1, source_target_pairs={{0,16},{1,17},{2,18},{3,19},{4,20},{5,21},{6,22},{7,23},{8,24},{9,... | collective-permute-start | bytes 393224 | tf_op jit(solution)/shard_map/ppermute | solution.py:51
  143.5 9.9 %collective-permute-start.29 = (bf16[640,256]{1,0:T(8,128)(2,1)S(1)}, bf16[640,256]{1,0:T(8,128)(2,1)S(1)}, u32[]{:S(2)}, u32[]{:S(2)}) collective-permute-start(bf16[640,256]{1,0:T(8,128)(2,1)S(1)} %get-tuple-element.95), channel_id=1, source_target_pairs={{0,8},{1,65},{2,10},{3,67},{4,12},{5,69},{6,14},{7,71},{8,0},{9,73... | collective-permute-start | bytes 983048 | tf_op jit(solution)/shard_map/ppermute | solution.py:51
  143.6 12.1 %collective-permute-start.30 = (bf16[640,256]{1,0:T(8,128)(2,1)S(1)}, bf16[640,256]{1,0:T(8,128)(2,1)S(1)}, u32[]{:S(2)}, u32[]{:S(2)}) collective-permute-start(bf16[640,256]{1,0:T(8,128)(2,1)S(1)} %get-tuple-element.96), channel_id=1, source_target_pairs={{0,4},{1,33},{2,6},{3,35},{4,8},{5,37},{6,10},{7,39},{8,12},{9,41}... | collective-permute-start | bytes 983048 | tf_op jit(solution)/shard_map/ppermute | solution.py:51
  148.3 8.6 %collective-permute-start.31 = (bf16[640,256]{1,0:T(8,128)(2,1)S(1)}, bf16[640,256]{1,0:T(8,128)(2,1)S(1)}, u32[]{:S(2)}, u32[]{:S(2)}) collective-permute-start(bf16[640,256]{1,0:T(8,128)(2,1)S(1)} %get-tuple-element.97), channel_id=1, source_target_pairs={{0,12},{1,97},{2,14},{3,99},{4,0},{5,101},{6,2},{7,103},{8,4},{9,1... | collective-permute-start | bytes 983048 | tf_op jit(solution)/shard_map/ppermute | solution.py:51
  148.6 10.9 %collective-permute-start.24 = (bf16[2,256,256]{2,1,0:T(8,128)(2,1)S(1)}, bf16[2,256,256]{2,1,0:T(8,128)(2,1)S(1)}, u32[]{:S(2)}, u32[]{:S(2)}) collective-permute-start(bf16[2,256,256]{2,1,0:T(8,128)(2,1)S(1)} %get-tuple-element.81), channel_id=1, source_target_pairs={{0,8},{1,65},{2,10},{3,67},{4,12},{5,69},{6,14},{7,71},{8,0},{9,73... | collective-permute-start | bytes 786440 | tf_op jit(solution)/shard_map/ppermute | solution.py:51
  150.8 11.8 %collective-permute-start.26 = (bf16[2,256,256]{2,1,0:T(8,128)(2,1)S(1)}, bf16[2,256,256]{2,1,0:T(8,128)(2,1)S(1)}, u32[]{:S(2)}, u32[]{:S(2)}) collective-permute-start(bf16[2,256,256]{2,1,0:T(8,128)(2,1)S(1)} %get-tuple-element.82), channel_id=1, source_target_pairs={{0,12},{1,97},{2,14},{3,99},{4,0},{5,101},{6,2},{7,103},{8,4},{9,1... | collective-permute-start | bytes 786440 | tf_op jit(solution)/shard_map/ppermute | solution.py:51
  153.4 9.1 %collective-permute-start.25 = (bf16[2,256,256]{2,1,0:T(8,128)(2,1)S(1)}, bf16[2,256,256]{2,1,0:T(8,128)(2,1)S(1)}, u32[]{:S(2)}, u32[]{:S(2)}) collective-permute-start(bf16[2,256,256]{2,1,0:T(8,128)(2,1)S(1)} %get-tuple-element.83), channel_id=1, source_target_pairs={{0,4},{1,33},{2,6},{3,35},{4,8},{5,37},{6,10},{7,39},{8,12},{9,41}... | collective-permute-start | bytes 786440 | tf_op jit(solution)/shard_map/ppermute | solution.py:51
  157.1 6.5 %collective-permute-start.32 = (bf16[2,256,256]{2,1,0:T(8,128)(2,1)S(1)}, bf16[2,256,256]{2,1,0:T(8,128)(2,1)S(1)}, u32[]{:S(2)}, u32[]{:S(2)}) collective-permute-start(bf16[2,256,256]{2,1,0:T(8,128)(2,1)S(1)} %fusion.1), channel_id=1, source_target_pairs={{0,16},{1,17},{2,18},{3,19},{4,20},{5,21},{6,22},{7,23},{8,24},{9,... | collective-permute-start | bytes 786440 | tf_op jit(solution)/shard_map/ppermute | solution.py:51
  157.4 1.4 collective-permute-start.33
